TPU v7x, 32 devices: a whole 2x2x4 slice. The times are simulated.
32 devices in a mesh: groups: 2 (over y), seq: 4 (over z), head: 2 (over x), sub: 2 (over core).
Axes of the slice: x: 2, y: 2, z: 4, core: 2. Of those that a mesh axis runs over, the one named last changes fastest.
Arguments:
- tokens: bfloat16 [4096, 3072], P(('groups', 'seq')), parts along dimension 0, may hold values from -6 to 6
- modulation: float32 [3, 3072], replicated, may hold values from -4 to 4
- w_qkv: bfloat16 [3072, 8, 768], P('seq', ('head', 'sub')), may hold values from -0.15625 to 0.15625
- w_out: bfloat16 [2048, 3072], P('seq', ('head', 'sub')), may hold values from -0.125 to 0.125
- pattern: int32 [32, 4], P(('groups', 'seq')), parts along dimension 0, may hold values from 0 to 15, as said below
- counts: int32 [32], P(('groups', 'seq')), parts along dimension 0, may hold values from 1 to 4, as said below
- spatial_mask: int32 [8, 4, 4], P(('groups', 'seq')), parts along dimension 0, may hold values from 0 to 1, as said below
Outputs:
- update: bfloat16 [4096, 3072], P(('groups', 'seq'), ('head', 'sub')), parts along dimension 0
There are 2 independent parts, one for each index of `groups`. A program takes and returns all parts, laid end to end along the dimension named above; an argument that names none is the same for every part. Nothing has to cross between parts.
Inputs may be any that keep to these rules, and one draw needn't show every extreme that they name: pattern[b, 0] = b; each further entry of row b is b plus a nonzero offset of size at most 2, the offsets of one row different, clipped to the blocks of the video. `counts`: blocks with a count above one all lie in one cyclic run of half of the 16 blocks. `spatial_mask`: every diagonal entry is 1.
All inputs are finite; a program needn't handle non-finite values.
Results may differ from a plain program's by a relative error of at most 0.012.
The roundings to bfloat16 on the way count: a program that leaves them out, or rounds other values in their place, can miss the bound.
Values may be sent and summed in bfloat16 or wider, within the bound.
A program may use at most 128 MiB of HBM per device.

v0:
```python
import functools
import math

import jax
import jax.numpy as jnp
from jax import lax
from jax.experimental import pallas as pl
from jax.experimental.pallas import tpu as pltpu
from jax.sharding import PartitionSpec as P

BLOCK = 128
WIN = 2


EPSILON = 1e-06


def with_halo(cells, sides, width):
    for axis, dim in sides:
        count = lax.axis_size(axis)
        ends = count - 1
        head = lax.slice_in_dim(cells, 0, width, axis=dim)
        tail = lax.slice_in_dim(cells, cells.shape[dim] - width, cells.shape[dim], axis=dim)
        cells = jnp.concatenate(
            [
                lax.ppermute(tail, axis, [(i, (i + 1) % count) for i in range(ends)]),
                cells,
                lax.ppermute(head, axis, [((i + 1) % count, i) for i in range(ends)]),
            ],
            axis=dim,
        )
    return cells


MESH = pl.DeviceIdType.MESH


def pieces_of(rows, most=4):
    for count in range(most, 0, -1):
        if rows % (16 * count) == 0:
            return count
    return 1


class LineGather:
    def __init__(self, own, slots, sems, chunks, count, parts):
        self.own, self.slots, self.chunks = own, slots, chunks
        self.sems, self.count, self.parts = sems, count, parts
        self.me = lax.axis_index("seq")
        self.group = lax.axis_index("groups")
        self.size = own.shape[0] // (parts * chunks)

    def rows(self, group, chunk):
        start = (group * self.chunks + chunk) * self.size
        return pl.ds(pl.multiple_of(start, self.size), self.size)

    def along(self, shard, chunk, way, own):
        rows = self.rows(self.group, chunk)
        source = self.own.at[rows] if own else self.slots.at[shard, rows]
        return pltpu.make_async_remote_copy(
            src_ref=source,
            dst_ref=self.slots.at[shard, rows],
            send_sem=self.sems.at[way, 0, shard, chunk],
            recv_sem=self.sems.at[way, 1, shard, chunk],
            device_id={"seq": self.me + (1 if way == 0 else -1)},
            device_id_type=MESH,
        )

    def across(self, shard, chunk, hop):
        rows = self.rows(self.group, chunk)
        return pltpu.make_async_remote_copy(
            src_ref=self.slots.at[shard, rows],
            dst_ref=self.slots.at[shard, rows],
            send_sem=self.sems.at[1 + hop, 0, shard, chunk],
            recv_sem=self.sems.at[1 + hop, 1, shard, chunk],
            device_id={"groups": lax.rem(self.group + hop, self.parts)},
            device_id_type=MESH,
        )

    def open_line(self):
        for chunk in range(self.chunks):
            for way in (0, 1):
                @pl.when(self.onward(way))
                def _():
                    self.along(self.me, chunk, way, True).start()

    def onward(self, way):
        return self.me < self.count - 1 if way == 0 else self.me > 0

    def shard_of(self, step, way):
        return self.me - step if way == 0 else self.me + step

    def present(self, step, way):
        return self.me >= step if way == 0 else self.me + step < self.count

    def relay(self, step):
        for chunk in range(self.chunks):
            for way in (0, 1):
                shard = self.shard_of(step, way)

                @pl.when(self.present(step, way))
                def _():
                    self.along(shard, chunk, way, False).wait_recv()

                    @pl.when(self.onward(way))
                    def _():
                        self.along(shard, chunk, way, False).start()

                    for hop in range(1, self.parts):
                        self.across(shard, chunk, hop).start()

    def complete(self, shard):
        for chunk in range(self.chunks):
            for hop in range(1, self.parts):
                self.across(shard, chunk, hop).wait_recv()

    def close_sends(self, step):
        for chunk in range(self.chunks):
            for way in (0, 1):
                shard = self.shard_of(step, way)

                @pl.when(self.present(step, way))
                def _():
                    @pl.when(self.onward(way))
                    def _():
                        self.along(shard, chunk, way, False).wait_send()

                    for hop in range(1, self.parts):
                        self.across(shard, chunk, hop).wait_send()

    def close_own(self):
        for chunk in range(self.chunks):
            for way in (0, 1):
                @pl.when(self.onward(way))
                def _():
                    self.along(self.me, chunk, way, True).wait_send()


def project_kernel(count, parts, q_chunks, o_chunks, hidden, w_own, o_own, qkv, o_all, slots, total, q_sems, o_sems, own_sem):
    me = lax.axis_index("seq")
    group = lax.axis_index("groups")
    barrier = pltpu.get_barrier_semaphore()

    @pl.when(me > 0)
    def _():
        pl.semaphore_signal(barrier, inc=1, device_id={"seq": me - 1}, device_id_type=MESH)

    @pl.when(me < count - 1)
    def _():
        pl.semaphore_signal(barrier, inc=1, device_id={"seq": me + 1}, device_id_type=MESH)

    for hop in range(1, parts):
        pl.semaphore_signal(
            barrier, inc=1, device_id={"groups": lax.rem(group + hop, parts)}, device_id_type=MESH
        )
    neighbours = jnp.where(me > 0, 1, 0) + jnp.where(me < count - 1, 1, 0) + (parts - 1)
    pl.semaphore_wait(barrier, neighbours)

    line = LineGather(w_own, slots, q_sems, q_chunks, count, parts)
    outs = LineGather(o_own, o_all, o_sems, o_chunks, count, parts)
    line.open_line()
    keep = pltpu.make_async_copy(o_own, o_all.at[me], own_sem)
    keep.start()
    tile = 256

    def add(shard, block, first):
        def column(j, carry):
            at = pl.ds(pl.multiple_of(j * tile, tile), tile)
            product = jnp.dot(hidden[shard], block[:, at], preferred_element_type=jnp.float32)
            total[:, at] = product if first else total[:, at] + product
            return carry

        lax.fori_loop(0, total.shape[1] // tile, column, 0)

    def finish(step):
        for way in (0, 1):
            shard = line.shard_of(step, way)

            @pl.when(line.present(step, way))
            def _():
                line.complete(shard)
                add(shard, slots.at[shard], False)

    add(me, w_own, True)

    def q_step(step, carry):
        line.relay(step)

        @pl.when(step > 1)
        def _():
            finish(step - 1)

        return carry

    lax.fori_loop(1, count, q_step, 0)
    outs.open_line()
    finish(count - 1)
    qkv[...] = total[...].astype(qkv.dtype)

    def o_step(step, carry):
        outs.relay(step)
        return carry

    lax.fori_loop(1, count, o_step, 0)

    def last(step, carry):
        line.close_sends(step)
        outs.close_sends(step)
        for way in (0, 1):
            shard = outs.shard_of(step, way)

            @pl.when(outs.present(step, way))
            def _():
                outs.complete(shard)

        return carry

    lax.fori_loop(1, count, last, 0)
    line.close_own()
    outs.close_own()
    keep.wait()


def project(hidden, w_own, o_own):
    count, parts = lax.axis_size("seq"), lax.axis_size("groups")
    rows, depth = hidden.shape
    hidden = hidden.reshape(rows, count, depth // count).transpose(1, 0, 2)
    width = w_own.shape[1]
    most = 4 if count <= 8 else 1
    q_chunks = pieces_of(w_own.shape[0] // parts, most)
    o_chunks = pieces_of(o_own.shape[0] // parts, most)
    vmem = pl.BlockSpec(memory_space=pltpu.VMEM)
    return pl.pallas_call(
        functools.partial(project_kernel, count, parts, q_chunks, o_chunks),
        out_shape=[
            jax.ShapeDtypeStruct((rows, width), jnp.bfloat16),
            jax.ShapeDtypeStruct((count,) + o_own.shape, jnp.bfloat16),
        ],
        in_specs=[vmem] * 3,
        out_specs=[vmem, pl.BlockSpec(memory_space=pl.ANY)],
        scratch_shapes=[
            pltpu.VMEM((count,) + w_own.shape, jnp.bfloat16),
            pltpu.VMEM((rows, width), jnp.float32),
            pltpu.SemaphoreType.DMA((1 + parts, 2, count, q_chunks)),
            pltpu.SemaphoreType.DMA((1 + parts, 2, count, o_chunks)),
            pltpu.SemaphoreType.DMA,
        ],
        compiler_params=pltpu.CompilerParams(
            collective_id=0, has_side_effects=True, vmem_limit_bytes=48 * 1024 * 1024
        ),
        name="project",
    )(hidden, w_own, o_own)


def mix_kernel(heads, subs, chunks, attn, w_all, gate, update, slots, total, x_sems, c_sems):
    head, sub = lax.axis_index("head"), lax.axis_index("sub")
    barrier = pltpu.get_barrier_semaphore()
    for hop in range(1, heads):
        pl.semaphore_signal(
            barrier, inc=1, device_id={"head": lax.rem(head + hop, heads)}, device_id_type=MESH
        )
    for hop in range(1, subs):
        pl.semaphore_signal(
            barrier, inc=1, device_id={"sub": lax.rem(sub + hop, subs)}, device_id_type=MESH
        )
    pl.semaphore_wait(barrier, heads + subs - 2)
    size = attn.shape[0] // chunks

    def to_head(hop, chunk):
        rows = pl.ds(chunk * size, size)
        return pltpu.make_async_remote_copy(
            src_ref=attn.at[rows],
            dst_ref=slots.at[hop, 0, rows],
            send_sem=x_sems.at[hop, 0, chunk],
            recv_sem=x_sems.at[hop, 1, chunk],
            device_id={"head": lax.rem(head + hop, heads)},
            device_id_type=MESH,
        )

    def to_sub(hop, turn, chunk):
        rows = pl.ds(chunk * size, size)
        return pltpu.make_async_remote_copy(
            src_ref=attn.at[rows] if hop == 0 else slots.at[hop, 0, rows],
            dst_ref=slots.at[hop, turn, rows],
            send_sem=c_sems.at[hop, turn, 0, chunk],
            recv_sem=c_sems.at[hop, turn, 1, chunk],
            device_id={"sub": lax.rem(sub + turn, subs)},
            device_id_type=MESH,
        )

    for chunk in range(chunks):
        for hop in range(1, heads):
            to_head(hop, chunk).start()
        for turn in range(1, subs):
            to_sub(0, turn, chunk).start()

    def add(chunk, hop, turn, first):
        rows = slice(chunk * size, (chunk + 1) * size)
        owner = lax.rem(head + heads - hop, heads) * subs + lax.rem(sub + subs - turn, subs)
        block = attn[rows, :] if hop == 0 and turn == 0 else slots[hop, turn, rows, :]
        product = jnp.dot(block, w_all[owner], preferred_element_type=jnp.float32)
        total[rows, :] = product if first else total[rows, :] + product

    for chunk in range(chunks):
        add(chunk, 0, 0, True)
    for chunk in range(chunks):
        for turn in range(1, subs):
            to_sub(0, turn, chunk).wait_recv()
            add(chunk, 0, turn, False)
    for chunk in range(chunks):
        for hop in range(1, heads):
            to_head(hop, chunk).wait_recv()
            for turn in range(1, subs):
                to_sub(hop, turn, chunk).start()
            add(chunk, hop, 0, False)
    for chunk in range(chunks):
        for hop in range(1, heads):
            for turn in range(1, subs):
                to_sub(hop, turn, chunk).wait_recv()
                add(chunk, hop, turn, False)
        rows = slice(chunk * size, (chunk + 1) * size)
        update[rows, :] = (gate[...] * total[rows, :]).astype(update.dtype)
    for chunk in range(chunks):
        for hop in range(1, heads):
            to_head(hop, chunk).wait_send()
        for hop in range(heads):
            for turn in range(1, subs):
                to_sub(hop, turn, chunk).wait_send()


def mix(attention, w_all, gate):
    heads, subs = lax.axis_size("head"), lax.axis_size("sub")
    rows, width = attention.shape
    chunks = pieces_of(rows, 2)
    vmem = pl.BlockSpec(memory_space=pltpu.VMEM)
    return pl.pallas_call(
        functools.partial(mix_kernel, heads, subs, chunks),
        out_shape=jax.ShapeDtypeStruct((rows, w_all.shape[-1]), jnp.bfloat16),
        in_specs=[vmem] * 3,
        out_specs=vmem,
        scratch_shapes=[
            pltpu.VMEM((heads, subs, rows, width), jnp.bfloat16),
            pltpu.VMEM((rows, w_all.shape[-1]), jnp.float32),
            pltpu.SemaphoreType.DMA((heads, 2, chunks)),
            pltpu.SemaphoreType.DMA((heads, subs, 2, chunks)),
        ],
        compiler_params=pltpu.CompilerParams(
            collective_id=1, has_side_effects=True, vmem_limit_bytes=40 * 1024 * 1024
        ),
        name="mix",
    )(attention, w_all, gate)


def modulate(tokens, modulation):
    values = tokens.astype(jnp.float32)
    center = jnp.mean(values, axis=-1, keepdims=True)
    spread = jnp.mean(jnp.square(values - center), axis=-1, keepdims=True)
    normed = (values - center) * lax.rsqrt(spread + EPSILON)
    return (normed * (1.0 + modulation[1]) + modulation[0]).astype(jnp.bfloat16)


def shards(tokens, modulation, w_qkv, w_out, pattern, counts, spatial_mask):
    row_count, feature_width = tokens.shape
    pairs_local = w_qkv.shape[1]
    head_size = w_qkv.shape[2] // 6
    frames_local = spatial_mask.shape[0]
    positions = row_count // frames_local
    slot_total = pattern.shape[1]
    scale_factor = 1.0 / math.sqrt(head_size)
    hidden = modulate(tokens, modulation)
    projected, whole_out = project(hidden, w_qkv.reshape(w_qkv.shape[0], -1), w_out)
    packed = projected.reshape(
        frames_local, positions, pairs_local, 6 * head_size
    )
    temporal_in = packed[..., : 3 * head_size].transpose(1, 0, 2, 3)
    received = lax.all_to_all(temporal_in, "seq", split_axis=0, concat_axis=1, tiled=True)
    position_span, frame_total, items, _ = received.shape
    relaid = received.reshape(position_span * frame_total, items, 3 * head_size)
    extended = with_halo(relaid[:, :, head_size:], (("seq", 0),), WIN * BLOCK)
    block_count = position_span * frame_total // BLOCK
    key_table = extended.reshape(block_count + 2 * WIN, BLOCK, items, 2 * head_size)
    queries = relaid[:, :, :head_size].reshape(block_count, BLOCK, items, head_size)
    offsets = pattern - (lax.axis_index("seq") * block_count - WIN)

    def slot_step(slot_index, state_pair):
        numerator, denominator = state_pair
        chosen = lax.dynamic_index_in_dim(offsets, slot_index, 1, keepdims=False)
        picked = jnp.take(key_table, chosen, axis=0)
        scores = (
            jnp.einsum(
                "bqnc,bknc->bnqk",
                queries,
                picked[..., :head_size],
                preferred_element_type=jnp.float32,
            )
            * scale_factor
        )
        alive = (slot_index < counts).astype(jnp.float32)
        weights = jnp.exp(scores) * alive[:, None, None, None]
        numerator = numerator + jnp.einsum(
            "bnqk,bknc->bnqc",
            weights.astype(jnp.bfloat16),
            picked[..., head_size:],
            preferred_element_type=jnp.float32,
        )
        return (numerator, denominator + jnp.sum(weights, axis=-1))

    start_state = (
        jnp.zeros((block_count, items, BLOCK, head_size), jnp.float32),
        jnp.zeros((block_count, items, BLOCK), jnp.float32),
    )
    numerator, denominator = lax.fori_loop(0, slot_total, slot_step, start_state)
    outcome = (numerator / denominator[..., None]).astype(jnp.bfloat16)
    outcome = outcome.transpose(0, 2, 1, 3).reshape(position_span, frame_total, items, head_size)
    temporal_out = lax.all_to_all(outcome, "seq", split_axis=1, concat_axis=0, tiled=True)
    spatial = packed[..., 3 * head_size :]
    blocks_frame = positions // BLOCK
    scores = (
        jnp.einsum(
            "fpnc,fqnc->fnpq",
            spatial[..., :head_size],
            spatial[..., head_size : 2 * head_size],
            preferred_element_type=jnp.float32,
        )
        * scale_factor
    )
    keep = spatial_mask.astype(jnp.float32)[:, None, :, None, :, None]
    weights = (
        jnp.exp(scores).reshape(frames_local, pairs_local, blocks_frame, BLOCK, blocks_frame, BLOCK)
        * keep
    )
    weights = weights.reshape(frames_local, pairs_local, positions, positions)
    denominator = jnp.sum(weights, axis=-1)
    numerator = jnp.einsum(
        "fnpq,fqnc->fpnc",
        weights.astype(jnp.bfloat16),
        spatial[..., 2 * head_size :],
        preferred_element_type=jnp.float32,
    )
    spatial_out = (numerator / denominator.transpose(0, 2, 1)[..., None]).astype(jnp.bfloat16)
    attention = jnp.concatenate([temporal_out.transpose(1, 0, 2, 3), spatial_out], axis=-1)
    attention = attention.reshape(row_count, pairs_local * 2 * head_size)
    out_width = w_out.shape[1]
    blocks = lax.axis_size("head") * lax.axis_size("sub")
    gate_slice = lax.dynamic_slice_in_dim(
        modulation[2], lax.axis_index(("head", "sub")) * out_width, out_width, 0
    )
    return mix(attention, whole_out.reshape(blocks, -1, out_width), gate_slice[None, :])

def meet(axes):
    barrier = pltpu.get_barrier_semaphore()
    others = 0
    for axis in axes:
        size = lax.axis_size(axis)
        for hop in range(1, size):
            other = lax.rem(lax.axis_index(axis) + hop, size)
            pl.semaphore_signal(barrier, inc=1, device_id={axis: other}, device_id_type=MESH)
            others += 1
    pl.semaphore_wait(barrier, others)


def push(source, target, send_sem, recv_sem, axis, place):
    return pltpu.make_async_remote_copy(
        src_ref=source,
        dst_ref=target,
        send_sem=send_sem,
        recv_sem=recv_sem,
        device_id={axis: place},
        device_id_type=MESH,
    )


def by_head_kernel(
    sizes, chunks, o_chunks, span, hid_own, w_own, o_own, lists, gate, update,
    hfull, wfull, blocks, o_all, lists_all, table, own, slots, total,
    w_sems, l_sems, z_sems, x_sems, c_sems, o_sems, own_sems, sz_sems, sx_sems, sc_sems,
):
    count, parts, heads, subs = sizes
    me, group = lax.axis_index("seq"), lax.axis_index("groups")
    head, sub = lax.axis_index("head"), lax.axis_index("sub")
    meet(("seq", "groups", "head", "sub"))
    quarter = hid_own.shape[0]
    size = quarter // chunks
    half = w_own.shape[0] // parts
    width = wfull.shape[2]
    mine = pl.ds(pl.multiple_of(group * half, half), half)

    def place(hop, axis, size_):
        return lax.rem(lax.axis_index(axis) + hop, size_)

    def source_of(hop):
        return lax.rem(me + count - hop, count)

    def w_part(other):
        return pl.ds(pl.multiple_of(other * width, width), width)

    def w_along(hop, shard):
        return push(
            w_own.at[mine, w_part(place(hop, "seq", count))], wfull.at[shard, mine],
            w_sems.at[0, 0, hop], w_sems.at[0, 1, hop], "seq", place(hop, "seq", count),
        )

    def w_across(hop, turn):
        spot = wfull.at[source_of(hop), mine]
        return push(
            spot, spot, w_sems.at[turn, 0, hop], w_sems.at[turn, 1, hop],
            "groups", place(turn, "groups", parts),
        )

    def l_along(hop):
        return push(
            lists, lists_all.at[me], l_sems.at[0, hop], l_sems.at[1, hop],
            "seq", place(hop, "seq", count),
        )

    def rows_of(head_hop, sub_hop, chunk):
        owner = lax.rem(head + heads - head_hop, heads) * subs + lax.rem(sub + subs - sub_hop, subs)
        return pl.ds(pl.multiple_of(owner * quarter + chunk * size, size), size)

    def spot(shard, head_hop, sub_hop, chunk):
        return hfull.at[shard, rows_of(head_hop, sub_hop, chunk)]

    def z_push(shard, chunk, way, own):
        target = spot(shard, 0, 0, chunk)
        return push(
            hid_own.at[pl.ds(chunk * size, size)] if own else target, target,
            z_sems.at[way, 0, shard, chunk], z_sems.at[way, 1, shard, chunk],
            "seq", me + (1 if way == 0 else -1),
        )

    def x_push(shard, chunk, hop, own=False):
        target = spot(shard, 0, 0, chunk)
        return push(
            hid_own.at[pl.ds(chunk * size, size)] if own else target, target,
            x_sems.at[hop, 0, shard, chunk], x_sems.at[hop, 1, shard, chunk],
            "head", place(hop, "head", heads),
        )

    def c_push(shard, chunk, hop, turn, own=False):
        target = spot(shard, hop, 0, chunk)
        return push(
            hid_own.at[pl.ds(chunk * size, size)] if own else target, target,
            c_sems.at[hop, turn, 0, shard, chunk], c_sems.at[hop, turn, 1, shard, chunk],
            "sub", place(turn, "sub", subs),
        )

    outs = LineGather(o_own, o_all, o_sems, o_chunks, count, parts)
    onward, shard_of, present = outs.onward, outs.shard_of, outs.present
    ways = lambda step: (0, 1) if step else (0,)

    for hop in range(1, count):
        l_along(hop).start()
    for hop in range(1, count):
        w_along(hop, me).start()
    for chunk in range(chunks):
        for way in (0, 1):
            @pl.when(onward(way))
            def _():
                z_push(me, chunk, way, True).start()
        for hop in range(1, heads):
            x_push(me, chunk, hop, True).start()
        for turn in range(1, subs):
            c_push(me, chunk, 0, turn, True).start()
    keeps = [
        pltpu.make_async_copy(o_own, o_all.at[me], own_sems.at[0]),
        pltpu.make_async_copy(w_own.at[:, w_part(me)], wfull.at[me], own_sems.at[1]),
        pltpu.make_async_copy(
            hid_own,
            hfull.at[me, pl.ds(pl.multiple_of((head * subs + sub) * quarter, quarter), quarter)],
            own_sems.at[2],
        ),
        pltpu.make_async_copy(lists, lists_all.at[me], own_sems.at[3]),
    ]
    for keep in keeps:
        keep.start()

    for hop in range(1, count):
        w_along(hop, source_of(hop)).wait_recv()
        for turn in range(1, parts):
            w_across(hop, turn).start()

    def z_relay(step):
        for chunk in range(chunks):
            for way in ways(step):
                shard = shard_of(step, way)

                @pl.when(present(step, way))
                def _():
                    z_push(shard, chunk, way, False).wait_recv()

                    @pl.when(onward(way))
                    def _():
                        z_push(shard, chunk, way, False).start()

                    for hop in range(1, heads):
                        x_push(shard, chunk, hop).start()
                    for turn in range(1, subs):
                        c_push(shard, chunk, 0, turn).start()

    def x_relay(step):
        for chunk in range(chunks):
            for way in ways(step):
                shard = shard_of(step, way)

                @pl.when(present(step, way))
                def _():
                    for hop in range(1, heads):
                        x_push(shard, chunk, hop).wait_recv()
                        for turn in range(1, subs):
                            c_push(shard, chunk, hop, turn).start()

    def finish(step):
        for way in ways(step):
            shard = shard_of(step, way)

            @pl.when(present(step, way))
            def _():
                for chunk in range(chunks):
                    for hop in range(heads):
                        for turn in range(1, subs):
                            c_push(shard, chunk, hop, turn).wait_recv()
                weight = wfull[...].reshape(-1, wfull.shape[-1])
                total = jnp.dot(hfull[shard], weight, preferred_element_type=jnp.float32)
                total = total.astype(blocks.dtype)
                rows = total.shape[0]

                @pl.when(lax.rem(me, 2) == 0)
                def _():
                    at = pl.ds(pl.multiple_of(shard * span, span), span)
                    for i in range(rows // span):
                        blocks[i, at, :] = total[i * span : (i + 1) * span]

                @pl.when(lax.rem(me, 2) == 1)
                def _():
                    each = blocks.shape[1]
                    for i in range(rows // each):
                        blocks[shard * (rows // each) + i] = total[i * each : (i + 1) * each]

    for step in range(1, count):
        z_relay(step)
        if step == count - 1:
            outs.open_line()
        if step == 2:
            for keep in keeps:
                keep.wait()
            for hop in range(1, count):
                for turn in range(1, parts):
                    w_across(hop, turn).wait_recv()
        if step >= 2:
            x_relay(step - 2)
            finish(step - 2)
    x_relay(count - 2)
    finish(count - 2)
    x_relay(count - 1)
    finish(count - 1)
    outs.relay(1)
    for hop in range(1, count):
        l_along(hop).wait_recv()
    to_table = pltpu.make_async_copy(lists_all, table, own_sems.at[4])
    to_table.start()
    to_table.wait()
    scale = 1.0 / math.sqrt(own.shape[2])
    attend(count, span, scale, lax.rem(me, 2), table, blocks, own)
    spread(
        count, heads, subs, outs, own, o_all, gate, update, slots, total,
        sz_sems, sx_sems, sc_sems, own_sems.at[5],
    )

    for hop in range(1, count):
        l_along(hop).wait_send()
        w_along(hop, me).wait_send()
        for turn in range(1, parts):
            w_across(hop, turn).wait_send()
    for step in range(count):
        for way in ways(step):
            shard = shard_of(step, way)

            @pl.when(present(step, way))
            def _():
                for chunk in range(chunks):
                    for side in (0, 1) if step == 0 else (way,):
                        @pl.when(onward(side))
                        def _():
                            z_push(shard, chunk, side, False).wait_send()
                    for hop in range(1, heads):
                        x_push(shard, chunk, hop).wait_send()
                    for hop in range(heads):
                        for turn in range(1, subs):
                            c_push(shard, chunk, hop, turn).wait_send()
    for step in range(1, count):
        outs.close_sends(step)
    outs.close_own()


def by_head(hid_own, w_own, o_own, lists, gate, span, block):
    sizes = tuple(lax.axis_size(axis) for axis in ("seq", "groups", "head", "sub"))
    count, parts, heads, subs = sizes
    rows = hid_own.shape[0] * heads * subs
    depth, width = hid_own.shape[1], w_own.shape[1] // count
    chunks = pieces_of(hid_own.shape[0], 4)
    o_chunks = pieces_of(o_own.shape[0] // parts, 2)
    vmem = pl.BlockSpec(memory_space=pltpu.VMEM)
    dma = pltpu.SemaphoreType.DMA
    return pl.pallas_call(
        functools.partial(by_head_kernel, sizes, chunks, o_chunks, span),
        out_shape=jax.ShapeDtypeStruct((rows, o_own.shape[1]), jnp.bfloat16),
        in_specs=[vmem] * 5,
        out_specs=vmem,
        scratch_shapes=[
            pltpu.VMEM((count, rows, depth), jnp.bfloat16),
            pltpu.VMEM((count, w_own.shape[0], width), jnp.bfloat16),
            pltpu.VMEM((count * rows // block, block, width), jnp.bfloat16),
            pltpu.VMEM((count,) + o_own.shape, jnp.bfloat16),
            pltpu.VMEM((count,) + lists.shape, lists.dtype),
            pltpu.SMEM((count,) + lists.shape, lists.dtype),
            pltpu.VMEM((count, rows, width // 3), jnp.bfloat16),
            pltpu.VMEM((heads, subs, rows, count * width // 3), jnp.bfloat16),
            pltpu.VMEM((rows, o_own.shape[1]), jnp.float32),
            dma((parts, 2, count)),
            dma((2, count)),
            dma((2, 2, count, chunks)),
            dma((heads, 2, count, chunks)),
            dma((heads, subs, 2, count, chunks)),
            dma((1 + parts, 2, count, o_chunks)),
            dma((6,)),
            dma((2, count)),
            dma((heads, 2, count)),
            dma((heads, subs, 2, count)),
        ],
        compiler_params=pltpu.CompilerParams(
            collective_id=2, has_side_effects=True, vmem_limit_bytes=56 * 1024 * 1024
        ),
        name="by_head",
    )(hid_own, w_own, o_own, lists, gate)


def attend(count, span, scale, role, table, blocks, out):
    total, block, width = blocks.shape
    size = width // 3
    each = total // count
    slots = each

    def query(b, carry):
        device, row = b // each, lax.rem(b, each)
        used = table[device, each, row]
        q = blocks[b, :, :size]
        numerator = jnp.zeros((block, size), jnp.float32)
        denominator = jnp.zeros((block, 1), jnp.float32)
        for j in range(slots):
            listed = table[device, row, j]
            seen = table[device, row, slots + j]
            at = jnp.where(role == 0, listed, device * each + j)
            alive = jnp.where(role == 0, jnp.where(j < used, 1.0, 0.0), jnp.where(seen > 0, 1.0, 0.0))
            scores = lax.dot_general(
                q, blocks[at, :, size : 2 * size], (((1,), (1,)), ((), ())),
                preferred_element_type=jnp.float32,
            )
            weights = jnp.exp(scores * scale) * alive
            denominator = denominator + jnp.sum(weights, axis=-1, keepdims=True)
            numerator = numerator + jnp.dot(
                weights.astype(jnp.bfloat16), blocks[at, :, 2 * size :],
                preferred_element_type=jnp.float32,
            )
        result = (numerator / denominator).astype(out.dtype)

        @pl.when(role == 0)
        def _():
            at = pl.ds(pl.multiple_of(b * span, span), span)
            for f in range(count):
                out[f, at, :] = result[f * span : (f + 1) * span]

        @pl.when(role == 1)
        def _():
            out[device, pl.ds(pl.multiple_of(row * block, block), block), :] = result

        return carry

    lax.fori_loop(0, total, query, 0, unroll=2)


def spread(
    count, heads, subs, outs, own, w_all, gate, update, slots, total, z_sems, x_sems, c_sems, own_sem
):
    me, head, sub = (lax.axis_index(axis) for axis in ("seq", "head", "sub"))
    size = own.shape[2]

    def columns(step):
        source = lax.rem(me + count - step, count)
        return pl.ds(pl.multiple_of(source * size, size), size)

    def spot(hop, turn, step):
        return slots.at[hop, turn, :, columns(step)]

    def to_seq(step):
        other = lax.rem(me + step, count)
        return push(
            own.at[other], spot(0, 0, 0), z_sems.at[0, step], z_sems.at[1, step], "seq", other
        )

    def to_head(hop, step):
        return push(
            own.at[me] if step == 0 else spot(0, 0, step), spot(hop, 0, step),
            x_sems.at[hop, 0, step], x_sems.at[hop, 1, step],
            "head", lax.rem(head + hop, heads),
        )

    def to_sub(hop, turn, step):
        return push(
            own.at[me] if hop == 0 and step == 0 else spot(hop, 0, step), spot(hop, turn, step),
            c_sems.at[hop, turn, 0, step], c_sems.at[hop, turn, 1, step],
            "sub", lax.rem(sub + turn, subs),
        )

    def hand_over(step):
        for hop in range(1, heads):
            to_head(hop, step).start()
        for turn in range(1, subs):
            to_sub(0, turn, step).start()

    def pass_on(step):
        for hop in range(1, heads):
            to_head(hop, step).wait_recv()
            for turn in range(1, subs):
                to_sub(hop, turn, step).start()

    for step in range(1, count):
        to_seq(step).start()
    hand_over(0)
    keep = pltpu.make_async_copy(own.at[me], spot(0, 0, 0), own_sem)
    keep.start()
    for step in range(1, count):
        if step > 1:
            outs.relay(step)
        to_seq(step).wait_recv()
        hand_over(step)
        pass_on(step - 1)
    keep.wait()

    def add(hop, turn, first):
        owner = lax.rem(head + heads - hop, heads) * subs + lax.rem(sub + subs - turn, subs)
        product = jnp.dot(slots[hop, turn], w_all[owner], preferred_element_type=jnp.float32)
        total[...] = product if first else total[...] + product

    pass_on(count - 1)
    for step in range(1, count):
        for way in (0, 1):
            @pl.when(outs.present(step, way))
            def _():
                outs.complete(outs.shard_of(step, way))
    add(0, 0, True)
    for hop in range(heads):
        if hop:
            add(hop, 0, False)
        for turn in range(1, subs):
            for step in range(count):
                to_sub(hop, turn, step).wait_recv()
            add(hop, turn, False)
    update[...] = (gate[...] * total[...]).astype(update.dtype)
    for step in range(count):
        if step:
            to_seq(step).wait_send()
        for hop in range(1, heads):
            to_head(hop, step).wait_send()
        for hop in range(heads):
            for turn in range(1, subs):
                to_sub(hop, turn, step).wait_send()


def modulate_kernel(tokens, modulation, hidden, held, sem):
    quarter = held.shape[0]
    place = lax.axis_index("head") * lax.axis_size("sub") + lax.axis_index("sub")
    rows = pl.ds(pl.multiple_of(place * quarter, quarter), quarter)
    fetch = pltpu.make_async_copy(tokens.at[rows], held, sem)
    fetch.start()
    fetch.wait()
    gain = 1.0 + modulation[1:2, :]
    shift = modulation[0:1, :]

    def some(i, carry):
        at = pl.ds(pl.multiple_of(i * 16, 16), 16)
        values = held[at, :].astype(jnp.float32)
        centered = values - jnp.mean(values, axis=-1, keepdims=True)
        spread_of = jnp.mean(jnp.square(centered), axis=-1, keepdims=True)
        normed = centered * lax.rsqrt(spread_of + EPSILON)
        hidden[at, :] = (normed * gain + shift).astype(hidden.dtype)
        return carry

    lax.fori_loop(0, quarter // 16, some, 0, unroll=4)


def modulate_part(tokens, modulation, quarter):
    vmem = pl.BlockSpec(memory_space=pltpu.VMEM)
    return pl.pallas_call(
        modulate_kernel,
        out_shape=jax.ShapeDtypeStruct((quarter, tokens.shape[1]), tokens.dtype),
        in_specs=[pl.BlockSpec(memory_space=pl.ANY), vmem],
        out_specs=vmem,
        scratch_shapes=[pltpu.VMEM((quarter, tokens.shape[1]), tokens.dtype), pltpu.SemaphoreType.DMA],
        name="modulate_part",
    )(tokens, modulation)


def shards_by_head(tokens, modulation, w_qkv, w_out, pattern, counts, spatial_mask):
    count = lax.axis_size("seq")
    blocks = lax.axis_size("head") * lax.axis_size("sub")
    row_count = tokens.shape[0]
    depth = w_qkv.shape[0]
    quarter = row_count // blocks
    place = lax.axis_index(("head", "sub"))
    span = BLOCK // count
    hid_own = modulate_part(tokens, modulation, quarter)
    each = counts.shape[0]
    lists = (
        jnp.pad(pattern, ((0, 8 - each), (0, 128 - each)))
        + jnp.pad(counts[None, :], ((each, 7 - each), (0, 128 - each)))
        + jnp.pad(spatial_mask[0], ((0, 8 - each), (each, 128 - 2 * each)))
    )
    out_width = w_out.shape[1]
    gate_slice = lax.dynamic_slice_in_dim(modulation[2], place * out_width, out_width, 0)
    return by_head(
        hid_own, w_qkv.reshape(depth, -1), w_out, lists, gate_slice[None, :], span, BLOCK
    )


def one_head_each(mesh_count, blocks, tokens, w_qkv, pattern, spatial_mask):
    rows, frames = tokens.shape[0], spatial_mask.shape[0]
    return (
        w_qkv.shape[1] * 2 == mesh_count > 2
        and frames == 1
        and mesh_count == blocks
        and pattern.shape[0] == pattern.shape[1] == spatial_mask.shape[1]
        and pattern.shape[0] < 8
        and spatial_mask.shape[2] == pattern.shape[1]
        and rows == BLOCK * spatial_mask.shape[1]
        and BLOCK % (16 * mesh_count) == 0
        and w_qkv.shape[0] % 128 == 0
        and rows % (16 * blocks) == 0
    )


def shards_any(*args):
    tokens, _, w_qkv, _, pattern, _, spatial_mask = args
    blocks = lax.axis_size("head") * lax.axis_size("sub")
    if one_head_each(lax.axis_size("seq"), blocks, tokens, w_qkv, pattern, spatial_mask):
        return shards_by_head(*args)
    return shards(*args)


def solution(mesh):
    return jax.shard_map(
        shards_any,
        mesh=mesh,
        in_specs=(
            P(("groups", "seq"), None),
            P(),
            P("seq", ("head", "sub"), None),
            P("seq", ("head", "sub")),
            P(("groups", "seq"), None),
            P(("groups", "seq")),
            P(("groups", "seq"), None, None),
        ),
        out_specs=P(("groups", "seq"), ("head", "sub")),
        check_vma=False,
    )
```

profile of v0, /device:TPU:25, one launch (start us, length us, event | category | flops | bytes accessed | tf_op | source)
XLA Modules:
  0.0 145.3 jit_solution(9022084067672620386)
XLA Ops:
  0.0 0.0 copy-start
  0.0 1.5 %pad_add_fusion.lists = s32[8,128]{1,0:T(8,128)} fusion(s32[4,4]{1,0:T(4,128)} %bitcast.6, s32[1,4]{1,0:T(1,128)} %bitcast.7, s32[4,4]{1,0:T(4,128)} %param.11), kind=kLoop, calls=%fused_computation | loop fusion | flops 2048 | bytes 4240 | tf_op jit(solution)/shard_map/add | solution.py:914
  1.5 0.8 slice.3
  2.3 0.6 constant_dynamic-slice_fusion.gate
  2.9 3.5 %modulate_part.1.hid_own = bf16[128,3072]{1,0:T(8,128)(2,1)} custom-call(bf16[512,3072]{1,0:T(8,128)(2,1)} %tokens.1, f32[3,3072]{1,0:T(4,128)} %modulation.1), custom_call_target="tpu_custom_call" | custom-call | tf_op jit(solution)/shard_map/modulate_part/pallas_call | solution.py:893
  6.4 0.0 copy-done
  6.4 1.8 %copy.8 = bf16[96,8,2,768]{3,1,2,0:T(8,128)(2,1)} copy(bf16[96,8,2,768]{3,2,1,0:T(2,128)(2,1)S(1)} %bitcast.5) | data formatting | bytes 4718592
  8.3 134.9 %by_head.1 = bf16[512,768]{1,0:T(8,128)(2,1)} custom-call(bf16[128,3072]{1,0:T(8,128)(2,1)} %modulate_part.1.hid_own, bf16[768,1536]{1,0:T(8,128)(2,1)} %bitcast.4, bf16[512,768]{1,0:T(8,128)(2,1)} %o_own.1, s32[8,128]{1,0:T(8,128)} %pad_add_fusion.lists, f32[1,768]{1,0:T(1,128)} %constant_dynamic-slice_fusion.gate), custom_call_target="tpu_custom_call" | custom-call | tf_op jit(solution)/shard_map/by_head/pallas_call | solution.py:704
  143.2 2.1 %copy.10 = bf16[512,768]{1,0:T(8,128)(2,1)} copy(bf16[512,768]{1,0:T(8,128)(2,1)} %by_head.1) | data formatting | bytes 1572864
Async XLA Ops:
  0.0 6.4 %copy-start = (bf16[768,2,768]{2,1,0:T(2,128)(2,1)S(1)}, bf16[768,2,768]{2,1,0:T(2,128)(2,1)}, u32[]{:S(2)}) copy-start(bf16[768,2,768]{2,1,0:T(2,128)(2,1)} %param.9) | copy-start | bytes 7077892
where the time goes:
time: 146 us; the launch traced here: 145 us
  Pallas kernels  138 us (95%)
  local copies, waits for them, and re-layouts  5.33 us (4%)
  other arithmetic  1.52 us (1%)
    pallas_call x1, Pallas kernels, by_head(): pl.pallas_call(functools.partial(by_head_kernel, sizes, chunks, o_chunks,...  135 us
    unnamed x4, local copies, waits for them, and re-layouts  3.91 us
    pallas_call x1, Pallas kernels, modulate_part(): pl.pallas_call(modulate_kernel, out_shape=jax.ShapeDtypeStruct((quarter,...  3.48 us

commit v1 on v0

v1 whole, which is shorter than its diff:
```python
import functools
import math

import jax
import jax.numpy as jnp
from jax import lax
from jax.experimental import pallas as pl
from jax.experimental.pallas import tpu as pltpu
from jax.sharding import PartitionSpec as P

BLOCK = 128
WIN = 2


EPSILON = 1e-06


def with_halo(cells, sides, width):
    for axis, dim in sides:
        count = lax.axis_size(axis)
        ends = count - 1
        head = lax.slice_in_dim(cells, 0, width, axis=dim)
        tail = lax.slice_in_dim(cells, cells.shape[dim] - width, cells.shape[dim], axis=dim)
        cells = jnp.concatenate(
            [
                lax.ppermute(tail, axis, [(i, (i + 1) % count) for i in range(ends)]),
                cells,
                lax.ppermute(head, axis, [((i + 1) % count, i) for i in range(ends)]),
            ],
            axis=dim,
        )
    return cells


MESH = pl.DeviceIdType.MESH


def pieces_of(rows, most=4):
    for count in range(most, 0, -1):
        if rows % (16 * count) == 0:
            return count
    return 1


class ShardLine:
    def __init__(self, own, slots, sems, chunks, count, parts):
        self.own, self.slots, self.chunks = own, slots, chunks
        self.sems, self.count, self.parts = sems, count, parts
        self.me = lax.axis_index("seq")
        self.group = lax.axis_index("groups")
        self.size = own.shape[0] // (parts * chunks)

    def rows(self, group, chunk):
        start = (group * self.chunks + chunk) * self.size
        return pl.ds(pl.multiple_of(start, self.size), self.size)

    def along(self, shard, chunk, way, own):
        rows = self.rows(self.group, chunk)
        source = self.own.at[rows] if own else self.slots.at[shard, rows]
        return pltpu.make_async_remote_copy(
            src_ref=source,
            dst_ref=self.slots.at[shard, rows],
            send_sem=self.sems.at[way, 0, shard, chunk],
            recv_sem=self.sems.at[way, 1, shard, chunk],
            device_id={"seq": self.me + (1 if way == 0 else -1)},
            device_id_type=MESH,
        )

    def across(self, shard, chunk, hop):
        rows = self.rows(self.group, chunk)
        return pltpu.make_async_remote_copy(
            src_ref=self.slots.at[shard, rows],
            dst_ref=self.slots.at[shard, rows],
            send_sem=self.sems.at[1 + hop, 0, shard, chunk],
            recv_sem=self.sems.at[1 + hop, 1, shard, chunk],
            device_id={"groups": lax.rem(self.group + hop, self.parts)},
            device_id_type=MESH,
        )

    def open_line(self):
        for chunk in range(self.chunks):
            for way in (0, 1):
                @pl.when(self.onward(way))
                def _():
                    self.along(self.me, chunk, way, True).start()

    def onward(self, way):
        return self.me < self.count - 1 if way == 0 else self.me > 0

    def shard_of(self, step, way):
        return self.me - step if way == 0 else self.me + step

    def present(self, step, way):
        return self.me >= step if way == 0 else self.me + step < self.count

    def relay(self, step):
        for chunk in range(self.chunks):
            for way in (0, 1):
                shard = self.shard_of(step, way)

                @pl.when(self.present(step, way))
                def _():
                    self.along(shard, chunk, way, False).wait_recv()

                    @pl.when(self.onward(way))
                    def _():
                        self.along(shard, chunk, way, False).start()

                    for hop in range(1, self.parts):
                        self.across(shard, chunk, hop).start()

    def complete(self, shard):
        for chunk in range(self.chunks):
            for hop in range(1, self.parts):
                self.across(shard, chunk, hop).wait_recv()

    def close_sends(self, step):
        for chunk in range(self.chunks):
            for way in (0, 1):
                shard = self.shard_of(step, way)

                @pl.when(self.present(step, way))
                def _():
                    @pl.when(self.onward(way))
                    def _():
                        self.along(shard, chunk, way, False).wait_send()

                    for hop in range(1, self.parts):
                        self.across(shard, chunk, hop).wait_send()

    def close_own(self):
        for chunk in range(self.chunks):
            for way in (0, 1):
                @pl.when(self.onward(way))
                def _():
                    self.along(self.me, chunk, way, True).wait_send()


def project_kernel(count, parts, q_chunks, o_chunks, hidden, w_own, o_own, qkv, o_all, slots, total, q_sems, o_sems, own_sem):
    me = lax.axis_index("seq")
    group = lax.axis_index("groups")
    barrier = pltpu.get_barrier_semaphore()

    @pl.when(me > 0)
    def _():
        pl.semaphore_signal(barrier, inc=1, device_id={"seq": me - 1}, device_id_type=MESH)

    @pl.when(me < count - 1)
    def _():
        pl.semaphore_signal(barrier, inc=1, device_id={"seq": me + 1}, device_id_type=MESH)

    for hop in range(1, parts):
        pl.semaphore_signal(
            barrier, inc=1, device_id={"groups": lax.rem(group + hop, parts)}, device_id_type=MESH
        )
    neighbours = jnp.where(me > 0, 1, 0) + jnp.where(me < count - 1, 1, 0) + (parts - 1)
    pl.semaphore_wait(barrier, neighbours)

    line = ShardLine(w_own, slots, q_sems, q_chunks, count, parts)
    outs = ShardLine(o_own, o_all, o_sems, o_chunks, count, parts)
    line.open_line()
    keep = pltpu.make_async_copy(o_own, o_all.at[me], own_sem)
    keep.start()
    tile = 256

    def add(shard, block, first):
        def column(j, carry):
            at = pl.ds(pl.multiple_of(j * tile, tile), tile)
            product = jnp.dot(hidden[shard], block[:, at], preferred_element_type=jnp.float32)
            total[:, at] = product if first else total[:, at] + product
            return carry

        lax.fori_loop(0, total.shape[1] // tile, column, 0)

    def finish(step):
        for way in (0, 1):
            shard = line.shard_of(step, way)

            @pl.when(line.present(step, way))
            def _():
                line.complete(shard)
                add(shard, slots.at[shard], False)

    add(me, w_own, True)

    def q_step(step, carry):
        line.relay(step)

        @pl.when(step > 1)
        def _():
            finish(step - 1)

        return carry

    lax.fori_loop(1, count, q_step, 0)
    outs.open_line()
    finish(count - 1)
    qkv[...] = total[...].astype(qkv.dtype)

    def o_step(step, carry):
        outs.relay(step)
        return carry

    lax.fori_loop(1, count, o_step, 0)

    def last(step, carry):
        line.close_sends(step)
        outs.close_sends(step)
        for way in (0, 1):
            shard = outs.shard_of(step, way)

            @pl.when(outs.present(step, way))
            def _():
                outs.complete(shard)

        return carry

    lax.fori_loop(1, count, last, 0)
    line.close_own()
    outs.close_own()
    keep.wait()


def project(hidden, w_own, o_own):
    count, parts = lax.axis_size("seq"), lax.axis_size("groups")
    rows, depth = hidden.shape
    hidden = hidden.reshape(rows, count, depth // count).transpose(1, 0, 2)
    width = w_own.shape[1]
    most = 4 if count <= 8 else 1
    q_chunks = pieces_of(w_own.shape[0] // parts, most)
    o_chunks = pieces_of(o_own.shape[0] // parts, most)
    vmem = pl.BlockSpec(memory_space=pltpu.VMEM)
    return pl.pallas_call(
        functools.partial(project_kernel, count, parts, q_chunks, o_chunks),
        out_shape=[
            jax.ShapeDtypeStruct((rows, width), jnp.bfloat16),
            jax.ShapeDtypeStruct((count,) + o_own.shape, jnp.bfloat16),
        ],
        in_specs=[vmem] * 3,
        out_specs=[vmem, pl.BlockSpec(memory_space=pl.ANY)],
        scratch_shapes=[
            pltpu.VMEM((count,) + w_own.shape, jnp.bfloat16),
            pltpu.VMEM((rows, width), jnp.float32),
            pltpu.SemaphoreType.DMA((1 + parts, 2, count, q_chunks)),
            pltpu.SemaphoreType.DMA((1 + parts, 2, count, o_chunks)),
            pltpu.SemaphoreType.DMA,
        ],
        compiler_params=pltpu.CompilerParams(
            collective_id=0, has_side_effects=True, vmem_limit_bytes=48 * 1024 * 1024
        ),
        name="project",
    )(hidden, w_own, o_own)


def mix_kernel(heads, subs, chunks, attn, w_all, gate, update, slots, total, x_sems, c_sems):
    head, sub = lax.axis_index("head"), lax.axis_index("sub")
    barrier = pltpu.get_barrier_semaphore()
    for hop in range(1, heads):
        pl.semaphore_signal(
            barrier, inc=1, device_id={"head": lax.rem(head + hop, heads)}, device_id_type=MESH
        )
    for hop in range(1, subs):
        pl.semaphore_signal(
            barrier, inc=1, device_id={"sub": lax.rem(sub + hop, subs)}, device_id_type=MESH
        )
    pl.semaphore_wait(barrier, heads + subs - 2)
    size = attn.shape[0] // chunks

    def to_head(hop, chunk):
        rows = pl.ds(chunk * size, size)
        return pltpu.make_async_remote_copy(
            src_ref=attn.at[rows],
            dst_ref=slots.at[hop, 0, rows],
            send_sem=x_sems.at[hop, 0, chunk],
            recv_sem=x_sems.at[hop, 1, chunk],
            device_id={"head": lax.rem(head + hop, heads)},
            device_id_type=MESH,
        )

    def to_sub(hop, turn, chunk):
        rows = pl.ds(chunk * size, size)
        return pltpu.make_async_remote_copy(
            src_ref=attn.at[rows] if hop == 0 else slots.at[hop, 0, rows],
            dst_ref=slots.at[hop, turn, rows],
            send_sem=c_sems.at[hop, turn, 0, chunk],
            recv_sem=c_sems.at[hop, turn, 1, chunk],
            device_id={"sub": lax.rem(sub + turn, subs)},
            device_id_type=MESH,
        )

    for chunk in range(chunks):
        for hop in range(1, heads):
            to_head(hop, chunk).start()
        for turn in range(1, subs):
            to_sub(0, turn, chunk).start()

    def add(chunk, hop, turn, first):
        rows = slice(chunk * size, (chunk + 1) * size)
        owner = lax.rem(head + heads - hop, heads) * subs + lax.rem(sub + subs - turn, subs)
        block = attn[rows, :] if hop == 0 and turn == 0 else slots[hop, turn, rows, :]
        product = jnp.dot(block, w_all[owner], preferred_element_type=jnp.float32)
        total[rows, :] = product if first else total[rows, :] + product

    for chunk in range(chunks):
        add(chunk, 0, 0, True)
    for chunk in range(chunks):
        for turn in range(1, subs):
            to_sub(0, turn, chunk).wait_recv()
            add(chunk, 0, turn, False)
    for chunk in range(chunks):
        for hop in range(1, heads):
            to_head(hop, chunk).wait_recv()
            for turn in range(1, subs):
                to_sub(hop, turn, chunk).start()
            add(chunk, hop, 0, False)
    for chunk in range(chunks):
        for hop in range(1, heads):
            for turn in range(1, subs):
                to_sub(hop, turn, chunk).wait_recv()
                add(chunk, hop, turn, False)
        rows = slice(chunk * size, (chunk + 1) * size)
        update[rows, :] = (gate[...] * total[rows, :]).astype(update.dtype)
    for chunk in range(chunks):
        for hop in range(1, heads):
            to_head(hop, chunk).wait_send()
        for hop in range(heads):
            for turn in range(1, subs):
                to_sub(hop, turn, chunk).wait_send()


def mix(attention, w_all, gate):
    heads, subs = lax.axis_size("head"), lax.axis_size("sub")
    rows, width = attention.shape
    chunks = pieces_of(rows, 2)
    vmem = pl.BlockSpec(memory_space=pltpu.VMEM)
    return pl.pallas_call(
        functools.partial(mix_kernel, heads, subs, chunks),
        out_shape=jax.ShapeDtypeStruct((rows, w_all.shape[-1]), jnp.bfloat16),
        in_specs=[vmem] * 3,
        out_specs=vmem,
        scratch_shapes=[
            pltpu.VMEM((heads, subs, rows, width), jnp.bfloat16),
            pltpu.VMEM((rows, w_all.shape[-1]), jnp.float32),
            pltpu.SemaphoreType.DMA((heads, 2, chunks)),
            pltpu.SemaphoreType.DMA((heads, subs, 2, chunks)),
        ],
        compiler_params=pltpu.CompilerParams(
            collective_id=1, has_side_effects=True, vmem_limit_bytes=40 * 1024 * 1024
        ),
        name="mix",
    )(attention, w_all, gate)


def modulate(tokens, modulation):
    values = tokens.astype(jnp.float32)
    center = jnp.mean(values, axis=-1, keepdims=True)
    spread = jnp.mean(jnp.square(values - center), axis=-1, keepdims=True)
    normed = (values - center) * lax.rsqrt(spread + EPSILON)
    return (normed * (1.0 + modulation[1]) + modulation[0]).astype(jnp.bfloat16)


def shards(tokens, modulation, w_qkv, w_out, pattern, counts, spatial_mask):
    row_count, feature_width = tokens.shape
    pairs_local = w_qkv.shape[1]
    head_size = w_qkv.shape[2] // 6
    frames_local = spatial_mask.shape[0]
    positions = row_count // frames_local
    slot_total = pattern.shape[1]
    scale_factor = 1.0 / math.sqrt(head_size)
    hidden = modulate(tokens, modulation)
    projected, whole_out = project(hidden, w_qkv.reshape(w_qkv.shape[0], -1), w_out)
    packed = projected.reshape(
        frames_local, positions, pairs_local, 6 * head_size
    )
    temporal_in = packed[..., : 3 * head_size].transpose(1, 0, 2, 3)
    received = lax.all_to_all(temporal_in, "seq", split_axis=0, concat_axis=1, tiled=True)
    position_span, frame_total, items, _ = received.shape
    relaid = received.reshape(position_span * frame_total, items, 3 * head_size)
    extended = with_halo(relaid[:, :, head_size:], (("seq", 0),), WIN * BLOCK)
    block_count = position_span * frame_total // BLOCK
    key_table = extended.reshape(block_count + 2 * WIN, BLOCK, items, 2 * head_size)
    queries = relaid[:, :, :head_size].reshape(block_count, BLOCK, items, head_size)
    offsets = pattern - (lax.axis_index("seq") * block_count - WIN)

    def slot_step(slot_index, state_pair):
        numerator, denominator = state_pair
        chosen = lax.dynamic_index_in_dim(offsets, slot_index, 1, keepdims=False)
        picked = jnp.take(key_table, chosen, axis=0)
        scores = (
            jnp.einsum(
                "bqnc,bknc->bnqk",
                queries,
                picked[..., :head_size],
                preferred_element_type=jnp.float32,
            )
            * scale_factor
        )
        alive = (slot_index < counts).astype(jnp.float32)
        weights = jnp.exp(scores) * alive[:, None, None, None]
        numerator = numerator + jnp.einsum(
            "bnqk,bknc->bnqc",
            weights.astype(jnp.bfloat16),
            picked[..., head_size:],
            preferred_element_type=jnp.float32,
        )
        return (numerator, denominator + jnp.sum(weights, axis=-1))

    start_state = (
        jnp.zeros((block_count, items, BLOCK, head_size), jnp.float32),
        jnp.zeros((block_count, items, BLOCK), jnp.float32),
    )
    numerator, denominator = lax.fori_loop(0, slot_total, slot_step, start_state)
    outcome = (numerator / denominator[..., None]).astype(jnp.bfloat16)
    outcome = outcome.transpose(0, 2, 1, 3).reshape(position_span, frame_total, items, head_size)
    temporal_out = lax.all_to_all(outcome, "seq", split_axis=1, concat_axis=0, tiled=True)
    spatial = packed[..., 3 * head_size :]
    blocks_frame = positions // BLOCK
    scores = (
        jnp.einsum(
            "fpnc,fqnc->fnpq",
            spatial[..., :head_size],
            spatial[..., head_size : 2 * head_size],
            preferred_element_type=jnp.float32,
        )
        * scale_factor
    )
    keep = spatial_mask.astype(jnp.float32)[:, None, :, None, :, None]
    weights = (
        jnp.exp(scores).reshape(frames_local, pairs_local, blocks_frame, BLOCK, blocks_frame, BLOCK)
        * keep
    )
    weights = weights.reshape(frames_local, pairs_local, positions, positions)
    denominator = jnp.sum(weights, axis=-1)
    numerator = jnp.einsum(
        "fnpq,fqnc->fpnc",
        weights.astype(jnp.bfloat16),
        spatial[..., 2 * head_size :],
        preferred_element_type=jnp.float32,
    )
    spatial_out = (numerator / denominator.transpose(0, 2, 1)[..., None]).astype(jnp.bfloat16)
    attention = jnp.concatenate([temporal_out.transpose(1, 0, 2, 3), spatial_out], axis=-1)
    attention = attention.reshape(row_count, pairs_local * 2 * head_size)
    out_width = w_out.shape[1]
    blocks = lax.axis_size("head") * lax.axis_size("sub")
    gate_slice = lax.dynamic_slice_in_dim(
        modulation[2], lax.axis_index(("head", "sub")) * out_width, out_width, 0
    )
    return mix(attention, whole_out.reshape(blocks, -1, out_width), gate_slice[None, :])

def push(source, target, send_sem, recv_sem, axis, place):
    return pltpu.make_async_remote_copy(
        src_ref=source,
        dst_ref=target,
        send_sem=send_sem,
        recv_sem=recv_sem,
        device_id={axis: place},
        device_id_type=MESH,
    )


def seats(count):
    return (count // 2 - 1, count // 2)


def by_pair_kernel(
    sizes, chunks, pieces, o_chunks,
    tokens, modulation, w_own, o_own, pattern, counts, mask, update,
    held, raw, stage, hfull, wfull, tq, sq, o_all, lists, lists_all, table, own, slots,
    tok_sems, l_sems, w_sems, z_sems, x_sems, c_sems, o_sems, keep_sems, sz_sems, sx_sems, sc_sems, own_sems,
):
    count, parts, heads, subs = sizes
    low, high = seats(count)
    me, group = lax.axis_index("seq"), lax.axis_index("groups")
    head, sub = lax.axis_index("head"), lax.axis_index("sub")
    other = low + high - me
    near = jnp.where(me == low, low - 1, high + 1)
    far = jnp.where(me == low, high + 1, low - 1)
    seated = jnp.logical_or(me == low, me == high)
    ended = jnp.logical_not(seated)
    outward = jnp.where(me == low, 1, 0)
    blocks = heads * subs
    quarter = held.shape[1]
    unit = quarter // chunks
    width = wfull.shape[2]
    half = w_own.shape[0] // parts
    piece = half // pieces
    block = unit * blocks

    barrier = pltpu.get_barrier_semaphore()
    others = 0
    for axis in ("seq", "groups", "head", "sub"):
        size = lax.axis_size(axis)
        for hop in range(1, size):
            partner = lax.rem(lax.axis_index(axis) + hop, size)
            pl.semaphore_signal(barrier, inc=1, device_id={axis: partner}, device_id_type=MESH)
            others += 1

    def rows_of(head_hop, sub_hop, chunk):
        owner = lax.rem(head + heads - head_hop, heads) * subs + lax.rem(sub + subs - sub_hop, subs)
        return pl.ds(pl.multiple_of((chunk * blocks + owner) * unit, unit), unit)

    def fetch(hop, chunk):
        return pltpu.make_async_copy(
            tokens.at[rows_of(hop, 0, chunk)], held.at[hop, pl.ds(chunk * unit, unit)],
            tok_sems.at[hop, chunk],
        )

    for chunk in range(chunks):
        fetch(0, chunk).start()
    raw_copy = pltpu.make_async_copy(w_own, raw, own_sems.at[0])
    raw_copy.start()
    o_copy = pltpu.make_async_copy(o_own, o_all.at[me], own_sems.at[1])
    o_copy.start()

    @pl.when(seated)
    def _():
        for hop in range(1, heads):
            for chunk in range(chunks):
                fetch(hop, chunk).start()

    lists[...] = jnp.zeros_like(lists)
    slots_of = pattern.shape[1]
    lists[0 : pattern.shape[0], 0:slots_of] = pattern[...]
    lists[8 : 8 + mask.shape[0], 0 : mask.shape[1]] = mask[...]
    lists[16:17, 0 : counts.shape[1]] = counts[...]
    gain = 1.0 + modulation[1:2, :]
    shift = modulation[0:1, :]

    def modulate_rows(hop):
        def some(i, carry):
            at = pl.ds(pl.multiple_of(i * 16, 16), 16)
            chunk = i // (unit // 16)
            owner = lax.rem(head + heads - hop, heads) * subs + sub
            start = (chunk * blocks + owner) * unit + lax.rem(i, unit // 16) * 16
            values = held[hop, at, :].astype(jnp.float32)
            centered = values - jnp.mean(values, axis=-1, keepdims=True)
            spread_of = jnp.mean(jnp.square(centered), axis=-1, keepdims=True)
            normed = centered * lax.rsqrt(spread_of + EPSILON)
            hfull[me, pl.ds(pl.multiple_of(start, 16), 16), :] = (normed * gain + shift).astype(hfull.dtype)
            return carry

        for chunk in range(chunks):
            fetch(hop, chunk).wait()
        lax.fori_loop(0, quarter // 16, some, 0, unroll=4)

    modulate_rows(0)
    pl.semaphore_wait(barrier, others)

    def spot(frame, head_hop, sub_hop, chunk):
        return hfull.at[frame, rows_of(head_hop, sub_hop, chunk)]

    def z_push(frame, chunk, place):
        target = spot(frame, 0, 0, chunk)
        return push(target, target, z_sems.at[0, frame, chunk], z_sems.at[1, frame, chunk], "seq", place)

    def x_push(frame, chunk, hop):
        target = spot(frame, 0, 0, chunk)
        return push(
            target, target, x_sems.at[hop, 0, frame, chunk], x_sems.at[hop, 1, frame, chunk],
            "head", lax.rem(head + hop, heads),
        )

    def c_push(frame, chunk, hop, turn):
        target = spot(frame, hop, 0, chunk)
        return push(
            target, target, c_sems.at[hop, turn, 0, frame, chunk], c_sems.at[hop, turn, 1, frame, chunk],
            "sub", lax.rem(sub + turn, subs),
        )

    def l_push(seat):
        return push(lists, lists_all.at[me], l_sems.at[0, seat - low], l_sems.at[1, me], "seq", seat)

    def w_rows(part, step):
        return pl.ds(pl.multiple_of(part * half + step * piece, piece), piece)

    def w_along(seat, source, step):
        return push(
            stage.at[seat - low, pl.ds(step * piece, piece)], wfull.at[source, w_rows(group, step)],
            w_sems.at[0, 0, seat - low, step], w_sems.at[0, 1, source, step], "seq", seat,
        )

    def w_across(source, step, turn):
        target = wfull.at[source, w_rows(group, step)]
        return push(
            target, target, w_sems.at[turn, 0, source, step], w_sems.at[turn, 1, source, step],
            "groups", lax.rem(group + turn, parts),
        )

    outs = LineGather(o_all, o_sems, o_chunks, count, parts)

    for seat in (low, high):
        @pl.when(me != seat)
        def _():
            l_push(seat).start()

    @pl.when(seated)
    def _():
        for chunk in range(chunks):
            z_push(me, chunk, other).start()
            for turn in range(1, subs):
                c_push(me, chunk, 0, turn).start()

    @pl.when(ended)
    def _():
        for chunk in range(chunks):
            z_push(me, chunk, jnp.where(me < low, low, high)).start()

    raw_copy.wait()

    def unpack(i, carry):
        start = pl.multiple_of(i * 64, 64)
        both = raw[pl.ds(pl.multiple_of(group * half + start, 64), 64)]
        first, second = both[:, 0, :], both[:, 1, :]
        stage[0, pl.ds(start, 64), :] = first
        stage[1, pl.ds(start, 64), :] = second
        return carry

    lax.fori_loop(0, half // 64, unpack, 0)

    @pl.when(seated)
    def _():
        for step in range(pieces):
            w_along(other, me, step).start()

    @pl.when(ended)
    def _():
        for seat in (jnp.where(me < low, high, low), jnp.where(me < low, low, high)):
            for step in range(pieces):
                w_along(seat, me, step).start()

    o_copy.wait()

    @pl.when(ended)
    def _():
        for way in (0, 1):
            outs.open_way(way)
        for step in range(1, count):
            for way in (0, 1):
                outs.relay(step, way)

    @pl.when(seated)
    def _():
        for way in (0, 1):
            @pl.when(outward == way)
            def _():
                outs.open_way(way)

        keep = pltpu.make_async_copy(lists, lists_all.at[me], own_sems.at[2])
        keep.start()
        for hop in range(1, heads):
            modulate_rows(hop)
            for chunk in range(chunks):
                for turn in range(1, subs):
                    c_push(me, chunk, hop, turn).start()

        def land(frame, chunk, onward):
            z_push(frame, chunk, other).wait_recv()
            for hop in range(1, heads):
                x_push(frame, chunk, hop).start()
            for turn in range(1, subs):
                c_push(frame, chunk, 0, turn).start()
            if onward:
                z_push(frame, chunk, other).start()

        def crossed(frame, chunk):
            for hop in range(1, heads):
                x_push(frame, chunk, hop).wait_recv()
                for turn in range(1, subs):
                    c_push(frame, chunk, hop, turn).start()

        def gathered(frame, chunk):
            for hop in range(heads):
                for turn in range(1, subs):
                    c_push(frame, chunk, hop, turn).wait_recv()

        def keep_pair(i, carry):
            at = pl.ds(pl.multiple_of(i * 64, 64), 64)
            both = raw[at]
            wfull[me, at, :] = jnp.where(me == low, both[:, 0, :], both[:, 1, :])
            return carry

        land(near, 0, True)
        land(other, 0, False)
        lax.fori_loop(0, w_own.shape[0] // 64, keep_pair, 0)
        for chunk in range(1, chunks):
            land(near, chunk, True)
            land(other, chunk, False)

        def w_land(source, step):
            w_along(me, source, step).wait_recv()
            for turn in range(1, parts):
                w_across(source, step, turn).start()

        marks = [(source, step) for step in range(pieces) for source in (other, far, near)]
        ahead = [(frame, chunk) for chunk in range(chunks) for frame in (near, other)]
        for i in range(max(len(marks), len(ahead))):
            if i < len(ahead):
                crossed(*ahead[i])
            if i < len(marks):
                w_land(*marks[i])

        for source in (near, other, far):
            l_push_from(lists_all, lists, l_sems, source, low, me).wait_recv()
        keep.wait()
        to_table = pltpu.make_async_copy(lists_all, table, own_sems.at[3])
        to_table.start()

        span = unit
        scale = math.log2(math.e) / math.sqrt(own.shape[2] // 2)
        size = own.shape[2] // 2
        total_blocks = tq.shape[0]
        each = total_blocks // count
        window = 2 * WIN + 1

        def project(frame, chunk):
            rows = pl.ds(pl.multiple_of(chunk * block, block), block)
            total = jnp.dot(
                hfull[frame, rows, :], wfull[...].reshape(-1, width), preferred_element_type=jnp.float32
            ).astype(tq.dtype)
            at = pl.ds(pl.multiple_of(frame * span, span), span)
            for i in range(blocks):
                tq[chunk * blocks + i, at, :] = total[i * span : (i + 1) * span, : 3 * size]
            sq[frame, rows, :] = total[:, 3 * size :]

        def project_frame(frame):
            lax.fori_loop(0, chunks, lambda chunk, carry: (project(frame, chunk), carry)[1], 0)

        def soft(q, keys, values, biases):
            scores = lax.dot_general(
                q, keys, (((1,), (1,)), ((), ())), preferred_element_type=jnp.float32
            )
            parts_of = []
            sums = None
            for i, bias in enumerate(biases):
                weight = jnp.exp2(scores[:, i * BLOCK : (i + 1) * BLOCK] * scale + bias)
                sums = weight if sums is None else sums + weight
                parts_of.append(weight.astype(jnp.bfloat16))
            numerator = jnp.dot(
                jnp.concatenate(parts_of, axis=1), values, preferred_element_type=jnp.float32
            )
            return (numerator / jnp.sum(sums, axis=-1, keepdims=True)).astype(own.dtype)

        def temporal(chunk):
            def query(i, carry):
                b = chunk * blocks + i
                device, row = b // each, lax.rem(b, each)
                start = jnp.clip(b - WIN, 0, total_blocks - window)
                used = table[device, 16, row]
                biases = []
                for w in range(window):
                    times = 0
                    for j in range(slots_of):
                        hit = jnp.logical_and(j < used, table[device, row, j] == start + w)
                        times = times + jnp.where(hit, 1, 0)
                    bias = jnp.float32(-jnp.inf)
                    for m in range(1, slots_of + 1):
                        bias = jnp.where(times == m, jnp.float32(math.log2(m)), bias)
                    biases.append(bias)
                near_by = pl.ds(start, window)
                result = soft(
                    tq[b, :, :size],
                    tq[near_by, :, size : 2 * size].reshape(-1, size),
                    tq[near_by, :, 2 * size :].reshape(-1, size),
                    biases,
                )
                at = pl.ds(pl.multiple_of(b * span, span), span)
                for f in range(count):
                    own[f, at, :size] = result[f * span : (f + 1) * span]
                return carry

            lax.fori_loop(0, blocks, query, 0)

        def spatial(frame):
            per = sq.shape[1] // BLOCK

            def query(i, carry):
                at = pl.ds(pl.multiple_of(i * BLOCK, BLOCK), BLOCK)
                biases = [
                    jnp.where(table[frame, 8 + i, j] > 0, jnp.float32(0), jnp.float32(-jnp.inf))
                    for j in range(per)
                ]
                own[frame, at, size:] = soft(
                    sq[frame, at, :size], sq[frame, :, size : 2 * size], sq[frame, :, 2 * size :], biases
                )
                return carry

            lax.fori_loop(0, per, query, 0)

        def send(frame, chunk):
            out_push(own, slots, sz_sems, me, frame, chunk, block, low).start()

        def settle(chunk):
            send(near, chunk)
            send(other, chunk)
            keep_out(own, slots, keep_sems, me, chunk, block, low).start()

        early = (me, near, other)
        for chunk in range(chunks + 1):
            if chunk < chunks:
                land(far, chunk, False)
            if chunk:
                crossed(far, chunk - 1)
            if chunk == 0:
                for source in (other, near, far):
                    for step in range(pieces):
                        for turn in range(1, parts):
                            w_across(source, step, turn).wait_recv()
                for earlier in range(chunks):
                    gathered(me, earlier)
                    gathered(near, earlier)
                    gathered(other, earlier)
                to_table.wait()
            if chunk < len(early):
                project_frame(early[chunk])
            if chunk and chunk <= len(early):
                spatial(early[chunk - 1])
            if chunk:
                gathered(far, chunk - 1)
                project(far, chunk - 1)
            if chunk == chunks - 2:
                for way in (0, 1):
                    @pl.when(outward != way)
                    def _():
                        outs.open_way(way)
            if chunk == chunks - 1:
                for way in (0, 1):
                    @pl.when(outward != way)
                    def _():
                        outs.relay(1, way)
            if chunk >= max(2, len(early)):
                for ready in range(chunk - 2 if chunk > max(2, len(early)) else 0, chunk - 1):
                    temporal(ready)
                    settle(ready)
        temporal(chunks - 1)
        settle(chunks - 1)
        spatial(far)
        for chunk in range(chunks):
            send(far, chunk)
        for way in (0, 1):
            @pl.when(outward == way)
            def _():
                outs.relay(1, way)
                outs.relay(2, way)

    columns_of = own.shape[2]

    def item(hop, turn, seat, chunk):
        return out_spot(slots, hop, turn, seat, chunk, block, low, columns_of)

    def to_head(hop, seat, chunk):
        return push(
            item(0, 0, seat, chunk), item(hop, 0, seat, chunk),
            sx_sems.at[hop, 0, seat - low, chunk], sx_sems.at[hop, 1, seat - low, chunk],
            "head", lax.rem(head + hop, heads),
        )

    def to_sub(hop, turn, seat, chunk):
        return push(
            item(hop, 0, seat, chunk), item(hop, turn, seat, chunk),
            sc_sems.at[hop, turn, 0, seat - low, chunk], sc_sems.at[hop, turn, 1, seat - low, chunk],
            "sub", lax.rem(sub + turn, subs),
        )

    def arrive(chunk, seat):
        @pl.when(me == seat)
        def _():
            keep_out(own, slots, keep_sems, seat, chunk, block, low).wait()

        @pl.when(me != seat)
        def _():
            out_push(own, slots, sz_sems, seat, me, chunk, block, low).wait_recv()

        for hop in range(1, heads):
            to_head(hop, seat, chunk).start()
        for turn in range(1, subs):
            to_sub(0, turn, seat, chunk).start()

    def pass_on(chunk, seat):
        for hop in range(1, heads):
            to_head(hop, seat, chunk).wait_recv()
            for turn in range(1, subs):
                to_sub(hop, turn, seat, chunk).start()

    columns = pl.ds(pl.multiple_of((head * subs + sub) * update.shape[1], 128), update.shape[1])
    gate = modulation[2:3, columns]

    def finish(chunk):
        for seat in (low, high):
            for hop in range(heads):
                for turn in range(1, subs):
                    to_sub(hop, turn, seat, chunk).wait_recv()
        rows = slice(chunk * block, (chunk + 1) * block)
        total = None
        for hop in range(heads):
            for turn in range(subs):
                owner = lax.rem(head + heads - hop, heads) * subs + lax.rem(sub + subs - turn, subs)
                product = jnp.dot(slots[hop, turn, rows, :], o_all[owner], preferred_element_type=jnp.float32)
                total = product if total is None else total + product
        update[rows, :] = (gate * total).astype(update.dtype)

    listed = [(chunk, seat) for chunk in range(chunks) for seat in (low, high)]
    for n, (chunk, seat) in enumerate(listed):
        arrive(chunk, seat)
        if n:
            pass_on(*listed[n - 1])
        if n == 2:
            for step in range(1, count):
                for way in (0, 1):
                    @pl.when(outs.present(step, way))
                    def _():
                        outs.complete(outs.shard_of(step, way))
        if chunk and seat == high:
            finish(chunk - 1)
    pass_on(*listed[-1])
    finish(chunks - 1)

    for seat in (low, high):
        @pl.when(me != seat)
        def _():
            l_push(seat).wait_send()
            for step in range(pieces):
                w_along(seat, me, step).wait_send()

    @pl.when(ended)
    def _():
        for chunk in range(chunks):
            z_push(me, chunk, jnp.where(me < low, low, high)).wait_send()

    @pl.when(seated)
    def _():
        for chunk in range(chunks):
            z_push(me, chunk, other).wait_send()
            z_push(near, chunk, other).wait_send()
            for frame in (me, near, other, far):
                for hop in range(heads):
                    for turn in range(1, subs):
                        c_push(frame, chunk, hop, turn).wait_send()
            for frame in (near, other, far):
                for hop in range(1, heads):
                    x_push(frame, chunk, hop).wait_send()
                out_push(own, slots, sz_sems, me, frame, chunk, block, low).wait_send()
        for source in (near, other, far):
            for step in range(pieces):
                for turn in range(1, parts):
                    w_across(source, step, turn).wait_send()

    for way in (0, 1):
        outs.close_way(way)
    for step in range(1, count):
        for way in (0, 1):
            outs.close_sends(step, way)
    for chunk in range(chunks):
        for seat in (low, high):
            for hop in range(1, heads):
                to_head(hop, seat, chunk).wait_send()
            for hop in range(heads):
                for turn in range(1, subs):
                    to_sub(hop, turn, seat, chunk).wait_send()


def l_push_from(lists_all, lists, l_sems, source, low, me):
    return push(lists, lists_all.at[source], l_sems.at[0, me - low], l_sems.at[1, source], "seq", me)


def out_spot(slots, hop, turn, seat, chunk, block, low, columns):
    at = (seat - low) * columns
    at = pl.ds(pl.multiple_of(at, columns), columns)
    return slots.at[hop, turn, pl.ds(chunk * block, block), at]


def out_push(own, slots, sems, seat, frame, chunk, block, low):
    return push(
        own.at[frame, pl.ds(chunk * block, block)],
        out_spot(slots, 0, 0, seat, chunk, block, low, own.shape[2]),
        sems.at[0, frame, chunk], sems.at[1, seat, chunk], "seq", frame,
    )


def keep_out(own, slots, sems, seat, chunk, block, low):
    return pltpu.make_async_copy(
        own.at[seat, pl.ds(chunk * block, block)],
        out_spot(slots, 0, 0, seat, chunk, block, low, own.shape[2]),
        sems.at[chunk],
    )


class LineGather:
    def __init__(self, slots, sems, chunks, count, parts):
        self.slots, self.chunks = slots, chunks
        self.sems, self.count, self.parts = sems, count, parts
        self.me = lax.axis_index("seq")
        self.group = lax.axis_index("groups")
        self.size = slots.shape[1] // (parts * chunks)

    def rows(self, group, chunk):
        start = (group * self.chunks + chunk) * self.size
        return pl.ds(pl.multiple_of(start, self.size), self.size)

    def along(self, shard, chunk, way):
        rows = self.rows(self.group, chunk)
        return push(
            self.slots.at[shard, rows], self.slots.at[shard, rows],
            self.sems.at[way, 0, shard, chunk], self.sems.at[way, 1, shard, chunk],
            "seq", self.me + (1 if way == 0 else -1),
        )

    def across(self, shard, chunk, hop):
        rows = self.rows(self.group, chunk)
        return push(
            self.slots.at[shard, rows], self.slots.at[shard, rows],
            self.sems.at[1 + hop, 0, shard, chunk], self.sems.at[1 + hop, 1, shard, chunk],
            "groups", lax.rem(self.group + hop, self.parts),
        )

    def onward(self, way):
        return self.me < self.count - 1 if way == 0 else self.me > 0

    def shard_of(self, step, way):
        return self.me - step if way == 0 else self.me + step

    def present(self, step, way):
        return self.me >= step if way == 0 else self.me + step < self.count

    def open_way(self, way):
        @pl.when(self.onward(way))
        def _():
            for chunk in range(self.chunks):
                self.along(self.me, chunk, way).start()

    def relay(self, step, way):
        shard = self.shard_of(step, way)

        @pl.when(self.present(step, way))
        def _():
            for chunk in range(self.chunks):
                self.along(shard, chunk, way).wait_recv()

                @pl.when(self.onward(way))
                def _():
                    self.along(shard, chunk, way).start()

                for hop in range(1, self.parts):
                    self.across(shard, chunk, hop).start()

    def complete(self, shard):
        for chunk in range(self.chunks):
            for hop in range(1, self.parts):
                self.across(shard, chunk, hop).wait_recv()

    def close_sends(self, step, way):
        shard = self.shard_of(step, way)

        @pl.when(self.present(step, way))
        def _():
            for chunk in range(self.chunks):
                @pl.when(self.onward(way))
                def _():
                    self.along(shard, chunk, way).wait_send()

                for hop in range(1, self.parts):
                    self.across(shard, chunk, hop).wait_send()

    def close_way(self, way):
        @pl.when(self.onward(way))
        def _():
            for chunk in range(self.chunks):
                self.along(self.me, chunk, way).wait_send()


def by_pair(tokens, modulation, w_own, o_own, pattern, counts, mask):
    sizes = tuple(lax.axis_size(axis) for axis in ("seq", "groups", "head", "sub"))
    count, parts, heads, subs = sizes
    rows, depth = tokens.shape
    width = w_own.shape[2]
    blocks = heads * subs
    quarter = rows // blocks
    chunks = rows // BLOCK
    pieces = 2
    o_chunks = 2
    columns = width // 3
    seated = len(seats(count))
    vmem = pl.BlockSpec(memory_space=pltpu.VMEM)
    whole = pl.BlockSpec(memory_space=pl.ANY)
    dma = pltpu.SemaphoreType.DMA
    kept = jnp.bfloat16
    return pl.pallas_call(
        functools.partial(by_pair_kernel, sizes, chunks, pieces, o_chunks),
        out_shape=jax.ShapeDtypeStruct((rows, o_own.shape[1]), kept),
        in_specs=[whole, vmem, whole, whole, vmem, vmem, vmem],
        out_specs=vmem,
        scratch_shapes=[
            pltpu.VMEM((heads, quarter, depth), kept),
            pltpu.VMEM(w_own.shape, kept),
            pltpu.VMEM((seated, w_own.shape[0] // parts, width), kept),
            pltpu.VMEM((count, rows, depth), kept),
            pltpu.VMEM((count, w_own.shape[0], width), kept),
            pltpu.VMEM((count * rows // BLOCK, BLOCK, width // 2), kept),
            pltpu.VMEM((count, rows, width // 2), kept),
            pltpu.VMEM((count,) + o_own.shape, kept),
            pltpu.VMEM((24, 128), jnp.int32),
            pltpu.VMEM((count, 24, 128), jnp.int32),
            pltpu.SMEM((count, 24, 128), jnp.int32),
            pltpu.VMEM((count, rows, columns), kept),
            pltpu.VMEM((heads, subs, rows, seated * columns), kept),
            dma((heads, chunks)),
            dma((2, count)),
            dma((parts, 2, count, pieces)),
            dma((2, count, chunks)),
            dma((heads, 2, count, chunks)),
            dma((heads, subs, 2, count, chunks)),
            dma((1 + parts, 2, count, o_chunks)),
            dma((chunks,)),
            dma((2, count, chunks)),
            dma((heads, 2, seated, chunks)),
            dma((heads, subs, 2, seated, chunks)),
            dma((4,)),
        ],
        compiler_params=pltpu.CompilerParams(
            collective_id=2, has_side_effects=True, vmem_limit_bytes=60 * 1024 * 1024
        ),
        name="by_pair",
    )(tokens, modulation, w_own, o_own, pattern, counts, mask)


def shards_by_pair(tokens, modulation, w_qkv, w_out, pattern, counts, spatial_mask):
    return by_pair(tokens, modulation, w_qkv, w_out, pattern, counts[None, :], spatial_mask[0])


def one_pair_each(count, blocks, parts, tokens, w_qkv, w_out, pattern, spatial_mask):
    rows, frames = tokens.shape[0], spatial_mask.shape[0]
    return (
        count == blocks == 4
        and w_qkv.shape[1] == len(seats(count))
        and frames == 1
        and rows == BLOCK * pattern.shape[0] == BLOCK * spatial_mask.shape[1]
        and pattern.shape[0] < 8
        and BLOCK % (16 * count) == 0
        and w_qkv.shape[0] % (128 * parts) == 0
        and w_out.shape[0] % (32 * parts) == 0
    )


def shards_any(*args):
    tokens, _, w_qkv, w_out, pattern, _, spatial_mask = args
    blocks = lax.axis_size("head") * lax.axis_size("sub")
    sizes = lax.axis_size("seq"), blocks, lax.axis_size("groups")
    if one_pair_each(*sizes, tokens, w_qkv, w_out, pattern, spatial_mask):
        return shards_by_pair(*args)
    return shards(*args)


def solution(mesh):
    return jax.shard_map(
        shards_any,
        mesh=mesh,
        in_specs=(
            P(("groups", "seq"), None),
            P(),
            P("seq", ("head", "sub"), None),
            P("seq", ("head", "sub")),
            P(("groups", "seq"), None),
            P(("groups", "seq")),
            P(("groups", "seq"), None, None),
        ),
        out_specs=P(("groups", "seq"), ("head", "sub")),
        check_vma=False,
    )
```

time: 146 us -> 158 us (1.082)
  the two profiles are of different devices: /device:TPU:25 before, /device:TPU:0 now
where the time goes in v1:
time: 158 us; the launch traced here: 157 us
  Pallas kernels  155 us (98%)
  local copies, waits for them, and re-layouts  2.06 us (1%)
    pallas_call x1, Pallas kernels, by_pair(): pl.pallas_call(functools.partial(by_pair_kernel, sizes, chunks, pieces, o...  155 us

profile of v1, /device:TPU:0, one launch (start us, length us, event | category | flops | bytes accessed | tf_op | source)
XLA Modules:
  0.0 157.5 jit_solution(14332685828614585522)
XLA Ops:
  0.0 155.4 %by_pair.1 = bf16[512,768]{1,0:T(8,128)(2,1)} custom-call(bf16[512,3072]{1,0:T(8,128)(2,1)} %tokens.1, f32[3,3072]{1,0:T(4,128)} %modulation.1, bf16[768,2,768]{2,1,0:T(2,128)(2,1)} %w_own.1, bf16[512,768]{1,0:T(8,128)(2,1)} %o_own.1, s32[4,4]{1,0:T(4,128)} %pattern.1, s32[1,4]{1,0:T(1,128)} %bitcast.3, s32[4,4]{1,0:T(4,128)} %bitcast.2), custom_call_target="tpu_custom_call" | custom-call | tf_op jit(solution)/shard_map/by_pair/pallas_call | solution.py:1086
  155.4 2.1 %copy.9 = bf16[512,768]{1,0:T(8,128)(2,1)} copy(bf16[512,768]{1,0:T(8,128)(2,1)} %by_pair.1) | data formatting | bytes 1572864

commit v2 on v1

--- a/solution.py
+++ b/solution.py
@@ -465,8 +465,8 @@
 def by_pair_kernel(
     sizes, chunks, pieces, o_chunks,
     tokens, modulation, w_own, o_own, pattern, counts, mask, update,
-    held, raw, stage, hfull, wfull, tq, sq, o_all, lists, lists_all, table, own, slots,
-    tok_sems, l_sems, w_sems, z_sems, x_sems, c_sems, o_sems, keep_sems, sz_sems, sx_sems, sc_sems, own_sems,
+    held, raw, stage, passing, partial, hfull, wfull, tq, sq, o_all, lists, lists_all, table, own, slots,
+    tok_sems, l_sems, w_sems, p_sems, z_sems, x_sems, c_sems, o_sems, keep_sems, sz_sems, sx_sems, sc_sems, own_sems,
 ):
     count, parts, heads, subs = sizes
     low, high = seats(count)
@@ -526,7 +526,7 @@
     gain = 1.0 + modulation[1:2, :]
     shift = modulation[0:1, :]
 
-    def modulate_rows(hop):
+    def modulate_rows(hop, first, last):
         def some(i, carry):
             at = pl.ds(pl.multiple_of(i * 16, 16), 16)
             chunk = i // (unit // 16)
@@ -539,11 +539,11 @@
             hfull[me, pl.ds(pl.multiple_of(start, 16), 16), :] = (normed * gain + shift).astype(hfull.dtype)
             return carry
 
-        for chunk in range(chunks):
+        for chunk in range(first, last):
             fetch(hop, chunk).wait()
-        lax.fori_loop(0, quarter // 16, some, 0, unroll=4)
-
-    modulate_rows(0)
+        lax.fori_loop(first * unit // 16, last * unit // 16, some, 0, unroll=2)
+
+    modulate_rows(0, 0, 1)
     pl.semaphore_wait(barrier, others)
 
     def spot(frame, head_hop, sub_hop, chunk):
@@ -579,6 +579,19 @@
             w_sems.at[0, 0, seat - low, step], w_sems.at[0, 1, source, step], "seq", seat,
         )
 
+    def w_hand(step, place):
+        return push(
+            stage.at[jnp.where(me < low, high, low) - low, pl.ds(step * piece, piece)],
+            passing.at[pl.ds(step * piece, piece)],
+            p_sems.at[0, step], p_sems.at[1, step], "seq", place,
+        )
+
+    def w_pass(source, step):
+        return push(
+            passing.at[pl.ds(step * piece, piece)], wfull.at[source, w_rows(group, step)],
+            w_sems.at[0, 0, me - low, step], w_sems.at[0, 1, source, step], "seq", other,
+        )
+
     def w_across(source, step, turn):
         target = wfull.at[source, w_rows(group, step)]
         return push(
@@ -593,18 +606,47 @@
         def _():
             l_push(seat).start()
 
-    @pl.when(seated)
-    def _():
-        for chunk in range(chunks):
-            z_push(me, chunk, other).start()
-            for turn in range(1, subs):
-                c_push(me, chunk, 0, turn).start()
-
-    @pl.when(ended)
-    def _():
-        for chunk in range(chunks):
-            z_push(me, chunk, jnp.where(me < low, low, high)).start()
-
+    columns_of = own.shape[2]
+
+    def item(hop, turn, seat, chunk):
+        return out_spot(slots, hop, turn, seat, chunk, block, low, columns_of)
+
+    def to_head(hop, seat, chunk, source=None):
+        return push(
+            item(0, 0, seat, chunk) if source is None else source, item(hop, 0, seat, chunk),
+            sx_sems.at[hop, 0, seat - low, chunk], sx_sems.at[hop, 1, seat - low, chunk],
+            "head", lax.rem(head + hop, heads),
+        )
+
+    def to_sub(hop, turn, seat, chunk, source=None):
+        return push(
+            item(hop, 0, seat, chunk) if source is None else source, item(hop, turn, seat, chunk),
+            sc_sems.at[hop, turn, 0, seat - low, chunk], sc_sems.at[hop, turn, 1, seat - low, chunk],
+            "sub", lax.rem(sub + turn, subs),
+        )
+
+    toward = jnp.where(me < low, low, high)
+
+    def relay_out(step, pieces_of_it, outgoing):
+        for way in (0, 1):
+            @pl.when((outward == way) == outgoing)
+            def _():
+                outs.relay(step, way, pieces_of_it)
+
+    o_first, o_last = tuple(range(o_chunks // 2)), tuple(range(o_chunks // 2, o_chunks))
+
+    def z_out(first, last):
+        @pl.when(seated)
+        def _():
+            for chunk in range(first, last):
+                z_push(me, chunk, other).start()
+
+        @pl.when(ended)
+        def _():
+            for chunk in range(first, last):
+                z_push(me, chunk, toward).start()
+
+    z_out(0, 1)
     raw_copy.wait()
 
     def unpack(i, carry):
@@ -617,26 +659,28 @@
 
     lax.fori_loop(0, half // 64, unpack, 0)
 
+    @pl.when(ended)
+    def _():
+        for step in range(pieces):
+            w_hand(step, toward).start()
+
     @pl.when(seated)
     def _():
         for step in range(pieces):
             w_along(other, me, step).start()
 
+    modulate_rows(0, 1, chunks)
+    o_copy.wait()
+
     @pl.when(ended)
     def _():
-        for seat in (jnp.where(me < low, high, low), jnp.where(me < low, low, high)):
-            for step in range(pieces):
-                w_along(seat, me, step).start()
-
-    o_copy.wait()
-
-    @pl.when(ended)
-    def _():
+        z_out(1, chunks)
+        for step in range(pieces):
+            w_along(toward, me, step).start()
         for way in (0, 1):
             outs.open_way(way)
-        for step in range(1, count):
-            for way in (0, 1):
-                outs.relay(step, way)
+        for way in (0, 1):
+            outs.relay(1, way)
 
     @pl.when(seated)
     def _():
@@ -647,20 +691,21 @@
 
         keep = pltpu.make_async_copy(lists, lists_all.at[me], own_sems.at[2])
         keep.start()
+        for chunk in range(chunks):
+            for turn in range(1, subs):
+                c_push(me, chunk, 0, turn).start()
         for hop in range(1, heads):
-            modulate_rows(hop)
+            modulate_rows(hop, 0, chunks)
             for chunk in range(chunks):
                 for turn in range(1, subs):
                     c_push(me, chunk, hop, turn).start()
 
-        def land(frame, chunk, onward):
+        def land(frame, chunk):
             z_push(frame, chunk, other).wait_recv()
             for hop in range(1, heads):
                 x_push(frame, chunk, hop).start()
             for turn in range(1, subs):
                 c_push(frame, chunk, 0, turn).start()
-            if onward:
-                z_push(frame, chunk, other).start()
 
         def crossed(frame, chunk):
             for hop in range(1, heads):
@@ -679,31 +724,10 @@
             wfull[me, at, :] = jnp.where(me == low, both[:, 0, :], both[:, 1, :])
             return carry
 
-        land(near, 0, True)
-        land(other, 0, False)
-        lax.fori_loop(0, w_own.shape[0] // 64, keep_pair, 0)
-        for chunk in range(1, chunks):
-            land(near, chunk, True)
-            land(other, chunk, False)
-
         def w_land(source, step):
             w_along(me, source, step).wait_recv()
             for turn in range(1, parts):
                 w_across(source, step, turn).start()
-
-        marks = [(source, step) for step in range(pieces) for source in (other, far, near)]
-        ahead = [(frame, chunk) for chunk in range(chunks) for frame in (near, other)]
-        for i in range(max(len(marks), len(ahead))):
-            if i < len(ahead):
-                crossed(*ahead[i])
-            if i < len(marks):
-                w_land(*marks[i])
-
-        for source in (near, other, far):
-            l_push_from(lists_all, lists, l_sems, source, low, me).wait_recv()
-        keep.wait()
-        to_table = pltpu.make_async_copy(lists_all, table, own_sems.at[3])
-        to_table.start()
 
         span = unit
         scale = math.log2(math.e) / math.sqrt(own.shape[2] // 2)
@@ -712,18 +736,102 @@
         each = total_blocks // count
         window = 2 * WIN + 1
 
+        depth = wfull.shape[1]
+
+        def first_part(frame, slot):
+            def some_rows(chunk, carry):
+                rows = pl.ds(pl.multiple_of(chunk * block, block), block)
+                partial[slot, rows, :] = jnp.dot(
+                    hfull[frame, rows, low * depth : (high + 1) * depth],
+                    wfull[low : high + 1].reshape(-1, width), preferred_element_type=jnp.float32,
+                )
+                return carry
+
+            lax.fori_loop(0, chunks, some_rows, 0)
+
+        def keep_qkv(frame, chunk, total):
+            at = pl.ds(pl.multiple_of(frame * span, span), span)
+            for i in range(blocks):
+                tq[chunk * blocks + i, at, :] = total[i * span : (i + 1) * span, : 3 * size]
+            sq[frame, pl.ds(pl.multiple_of(chunk * block, block), block), :] = total[:, 3 * size :]
+
+        land(near, 0)
+        land(other, 0)
+        for step in range(pieces):
+            w_hand(step, other).wait_recv()
+            w_pass(near, step).start()
+            w_land(other, step)
+        for chunk in range(1, chunks):
+            z_push(me, chunk, other).start()
+        z_push(near, 0, other).start()
+        crossed(near, 0)
+        crossed(other, 0)
+        lax.fori_loop(0, w_own.shape[0] // 64, keep_pair, 0)
+        rest = max(pieces, chunks - 1)
+        for i in range(rest):
+            if i + 1 < chunks:
+                land(near, i + 1)
+                z_push(near, i + 1, other).start()
+            if i < pieces:
+                w_land(far, i)
+        for way in (0, 1):
+            @pl.when(outward != way)
+            def _():
+                outs.open_way(way)
+        def crossed_w(source):
+            for step in range(pieces):
+                for turn in range(1, parts):
+                    w_across(source, step, turn).wait_recv()
+
+        def all_in(frame):
+            for chunk in range(chunks):
+                gathered(frame, chunk)
+
+        crossed_w(other)
+        all_in(me)
+        first_part(me, 0)
+        for i in range(rest):
+            if i + 1 < chunks:
+                land(other, i + 1)
+            if i < pieces:
+                w_land(near, i)
+            if i + 1 < chunks:
+                crossed(near, i + 1)
+            if i == rest - 1:
+                all_in(near)
+                first_part(near, 1)
+        for i in range(1, chunks):
+            crossed(other, i)
+        land(far, 0)
+        all_in(other)
+        first_part(other, 2)
+
+        for source in (near, other, far):
+            l_push_from(lists_all, lists, l_sems, source, low, me).wait_recv()
+        keep.wait()
+        to_table = pltpu.make_async_copy(lists_all, table, own_sems.at[3])
+        to_table.start()
+
         def project(frame, chunk):
             rows = pl.ds(pl.multiple_of(chunk * block, block), block)
             total = jnp.dot(
                 hfull[frame, rows, :], wfull[...].reshape(-1, width), preferred_element_type=jnp.float32
             ).astype(tq.dtype)
-            at = pl.ds(pl.multiple_of(frame * span, span), span)
-            for i in range(blocks):
-                tq[chunk * blocks + i, at, :] = total[i * span : (i + 1) * span, : 3 * size]
-            sq[frame, rows, :] = total[:, 3 * size :]
-
-        def project_frame(frame):
-            lax.fori_loop(0, chunks, lambda chunk, carry: (project(frame, chunk), carry)[1], 0)
+            keep_qkv(frame, chunk, total)
+
+        def project_frame(frame, slot):
+            def last_part(chunk, carry):
+                rows = pl.ds(pl.multiple_of(chunk * block, block), block)
+                total = partial[slot, rows, :]
+                for source in (0, count - 1):
+                    at = slice(source * depth, (source + 1) * depth)
+                    total = total + jnp.dot(
+                        hfull[frame, rows, at], wfull[source], preferred_element_type=jnp.float32
+                    )
+                keep_qkv(frame, chunk, total.astype(tq.dtype))
+                return carry
+
+            lax.fori_loop(0, chunks, last_part, 0)
 
         def soft(q, keys, values, biases):
             scores = lax.dot_general(
@@ -793,83 +901,49 @@
             send(near, chunk)
             send(other, chunk)
             keep_out(own, slots, keep_sems, me, chunk, block, low).start()
+            mine = own.at[me, pl.ds(chunk * block, block)]
+            for hop in range(1, heads):
+                to_head(hop, me, chunk, mine).start()
+            for turn in range(1, subs):
+                to_sub(0, turn, me, chunk, mine).start()
 
         early = (me, near, other)
         for chunk in range(chunks + 1):
-            if chunk < chunks:
-                land(far, chunk, False)
-            if chunk:
+            if 0 < chunk < chunks:
+                land(far, chunk)
+            if chunk and chunk < chunks:
                 crossed(far, chunk - 1)
             if chunk == 0:
-                for source in (other, near, far):
-                    for step in range(pieces):
-                        for turn in range(1, parts):
-                            w_across(source, step, turn).wait_recv()
-                for earlier in range(chunks):
-                    gathered(me, earlier)
-                    gathered(near, earlier)
-                    gathered(other, earlier)
+                crossed_w(far)
+                crossed_w(near)
                 to_table.wait()
             if chunk < len(early):
-                project_frame(early[chunk])
+                project_frame(early[chunk], chunk)
             if chunk and chunk <= len(early):
                 spatial(early[chunk - 1])
             if chunk:
                 gathered(far, chunk - 1)
                 project(far, chunk - 1)
-            if chunk == chunks - 2:
-                for way in (0, 1):
-                    @pl.when(outward != way)
-                    def _():
-                        outs.open_way(way)
+            if chunk == 1:
+                relay_out(1, None, False)
             if chunk == chunks - 1:
-                for way in (0, 1):
-                    @pl.when(outward != way)
-                    def _():
-                        outs.relay(1, way)
-            if chunk >= max(2, len(early)):
-                for ready in range(chunk - 2 if chunk > max(2, len(early)) else 0, chunk - 1):
+                relay_out(1, o_first, True)
+                crossed(far, chunks - 1)
+                for ready in range(chunks - 2):
                     temporal(ready)
                     settle(ready)
-        temporal(chunks - 1)
-        settle(chunks - 1)
+                relay_out(1, o_last, True)
+        for ready in (chunks - 2, chunks - 1):
+            temporal(ready)
+            settle(ready)
+        relay_out(2, o_first, True)
         spatial(far)
         for chunk in range(chunks):
             send(far, chunk)
-        for way in (0, 1):
-            @pl.when(outward == way)
-            def _():
-                outs.relay(1, way)
-                outs.relay(2, way)
-
-    columns_of = own.shape[2]
-
-    def item(hop, turn, seat, chunk):
-        return out_spot(slots, hop, turn, seat, chunk, block, low, columns_of)
-
-    def to_head(hop, seat, chunk):
-        return push(
-            item(0, 0, seat, chunk), item(hop, 0, seat, chunk),
-            sx_sems.at[hop, 0, seat - low, chunk], sx_sems.at[hop, 1, seat - low, chunk],
-            "head", lax.rem(head + hop, heads),
-        )
-
-    def to_sub(hop, turn, seat, chunk):
-        return push(
-            item(hop, 0, seat, chunk), item(hop, turn, seat, chunk),
-            sc_sems.at[hop, turn, 0, seat - low, chunk], sc_sems.at[hop, turn, 1, seat - low, chunk],
-            "sub", lax.rem(sub + turn, subs),
-        )
+        relay_out(2, o_last, True)
 
     def arrive(chunk, seat):
-        @pl.when(me == seat)
-        def _():
-            keep_out(own, slots, keep_sems, seat, chunk, block, low).wait()
-
-        @pl.when(me != seat)
-        def _():
-            out_push(own, slots, sz_sems, seat, me, chunk, block, low).wait_recv()
-
+        out_push(own, slots, sz_sems, seat, me, chunk, block, low).wait_recv()
         for hop in range(1, heads):
             to_head(hop, seat, chunk).start()
         for turn in range(1, subs):
@@ -898,36 +972,70 @@
                 total = product if total is None else total + product
         update[rows, :] = (gate * total).astype(update.dtype)
 
-    listed = [(chunk, seat) for chunk in range(chunks) for seat in (low, high)]
-    for n, (chunk, seat) in enumerate(listed):
-        arrive(chunk, seat)
-        if n:
-            pass_on(*listed[n - 1])
-        if n == 2:
-            for step in range(1, count):
-                for way in (0, 1):
-                    @pl.when(outs.present(step, way))
-                    def _():
-                        outs.complete(outs.shard_of(step, way))
-        if chunk and seat == high:
-            finish(chunk - 1)
-    pass_on(*listed[-1])
-    finish(chunks - 1)
+    nearer = jnp.where(seated, me, toward)
+    farther = low + high - nearer
+    def relay_end(step, pieces_of_it):
+        for way in (0, 1):
+            outs.relay(step, way, pieces_of_it)
+
+    @pl.when(ended)
+    def _():
+        relay_end(2, None)
+        for chunk in range(chunks):
+            arrive(chunk, nearer)
+            if chunk:
+                pass_on(chunk - 1, nearer)
+            if chunk == chunks // 2 - 1:
+                relay_end(3, o_first)
+        pass_on(chunks - 1, nearer)
+
+    @pl.when(seated)
+    def _():
+        for chunk in range(chunks):
+            pass_on(chunk, nearer)
+
+    for chunk in range(chunks):
+        arrive(chunk, farther)
+        if chunk:
+            pass_on(chunk - 1, farther)
+        if chunk < len(o_last):
+            @pl.when(ended)
+            def _():
+                relay_end(3, o_last[chunk : chunk + 1])
+
+    pass_on(chunks - 1, farther)
+
+    @pl.when(seated)
+    def _():
+        for chunk in range(chunks):
+            keep_out(own, slots, keep_sems, me, chunk, block, low).wait()
+
+    for step in range(1, count):
+        for way in (0, 1):
+            @pl.when(outs.present(step, way))
+            def _():
+                outs.complete(outs.shard_of(step, way))
+    for chunk in range(chunks):
+        finish(chunk)
 
     for seat in (low, high):
         @pl.when(me != seat)
         def _():
             l_push(seat).wait_send()
-            for step in range(pieces):
-                w_along(seat, me, step).wait_send()
 
     @pl.when(ended)
     def _():
+        for step in range(pieces):
+            w_hand(step, toward).wait_send()
+            w_along(toward, me, step).wait_send()
         for chunk in range(chunks):
             z_push(me, chunk, jnp.where(me < low, low, high)).wait_send()
 
     @pl.when(seated)
     def _():
+        for step in range(pieces):
+            w_along(other, me, step).wait_send()
+            w_pass(near, step).wait_send()
         for chunk in range(chunks):
             z_push(me, chunk, other).wait_send()
             z_push(near, chunk, other).wait_send()
@@ -1027,12 +1135,12 @@
             for chunk in range(self.chunks):
                 self.along(self.me, chunk, way).start()
 
-    def relay(self, step, way):
+    def relay(self, step, way, chunks=None):
         shard = self.shard_of(step, way)
 
         @pl.when(self.present(step, way))
         def _():
-            for chunk in range(self.chunks):
+            for chunk in range(self.chunks) if chunks is None else chunks:
                 self.along(shard, chunk, way).wait_recv()
 
                 @pl.when(self.onward(way))
@@ -1075,8 +1183,8 @@
     blocks = heads * subs
     quarter = rows // blocks
     chunks = rows // BLOCK
-    pieces = 2
-    o_chunks = 2
+    pieces = 3
+    o_chunks = 4
     columns = width // 3
     seated = len(seats(count))
     vmem = pl.BlockSpec(memory_space=pltpu.VMEM)
@@ -1092,6 +1200,8 @@
             pltpu.VMEM((heads, quarter, depth), kept),
             pltpu.VMEM(w_own.shape, kept),
             pltpu.VMEM((seated, w_own.shape[0] // parts, width), kept),
+            pltpu.VMEM((w_own.shape[0] // parts, width), kept),
+            pltpu.VMEM((count - 1, rows, width), jnp.float32),
             pltpu.VMEM((count, rows, depth), kept),
             pltpu.VMEM((count, w_own.shape[0], width), kept),
             pltpu.VMEM((count * rows // BLOCK, BLOCK, width // 2), kept),
@@ -1105,6 +1215,7 @@
             dma((heads, chunks)),
             dma((2, count)),
             dma((parts, 2, count, pieces)),
+            dma((2, pieces)),
             dma((2, count, chunks)),
             dma((heads, 2, count, chunks)),
             dma((heads, subs, 2, count, chunks)),
@@ -1135,8 +1246,8 @@
         and rows == BLOCK * pattern.shape[0] == BLOCK * spatial_mask.shape[1]
         and pattern.shape[0] < 8
         and BLOCK % (16 * count) == 0
-        and w_qkv.shape[0] % (128 * parts) == 0
-        and w_out.shape[0] % (32 * parts) == 0
+        and w_qkv.shape[0] % (192 * parts) == 0
+        and w_out.shape[0] % (64 * parts) == 0
     )
 
 

time: 158 us -> 127 us (0.80)
  Pallas kernels: 155 us -> 124 us
    pallas_call x1, Pallas kernels: 155 us -> 124 us  [by_pair(): pl.pallas_call(functools.partial(by_pair_kernel, sizes, chunks, pieces, o...]
where the time goes in v2:
time: 127 us
  Pallas kernels  124 us (98%)
  local copies, waits for them, and re-layouts  2.06 us (2%)
    pallas_call x1, Pallas kernels, by_pair(): pl.pallas_call(functools.partial(by_pair_kernel, sizes, chunks, pieces, o...  124 us

profile of v2, /device:TPU:0, one launch (start us, length us, event | category | flops | bytes accessed | tf_op | source)
XLA Modules:
  0.0 126.6 jit_solution(16214009441606161391)
XLA Ops:
  0.0 124.5 %by_pair.1 = bf16[512,768]{1,0:T(8,128)(2,1)} custom-call(bf16[512,3072]{1,0:T(8,128)(2,1)} %tokens.1, f32[3,3072]{1,0:T(4,128)} %modulation.1, bf16[768,2,768]{2,1,0:T(2,128)(2,1)} %w_own.1, bf16[512,768]{1,0:T(8,128)(2,1)} %o_own.1, s32[4,4]{1,0:T(4,128)} %pattern.1, s32[1,4]{1,0:T(1,128)} %bitcast.3, s32[4,4]{1,0:T(4,128)} %bitcast.2), custom_call_target="tpu_custom_call" | custom-call | tf_op jit(solution)/shard_map/by_pair/pallas_call | solution.py:1194
  124.5 2.1 %copy.9 = bf16[512,768]{1,0:T(8,128)(2,1)} copy(bf16[512,768]{1,0:T(8,128)(2,1)} %by_pair.1) | data formatting | bytes 1572864

commit v3 on v2

--- a/solution.py
+++ b/solution.py
@@ -913,6 +913,8 @@
                 land(far, chunk)
             if chunk and chunk < chunks:
                 crossed(far, chunk - 1)
+            if chunk == chunks - 2:
+                relay_out(1, o_first[:1], True)
             if chunk == 0:
                 crossed_w(far)
                 crossed_w(near)
@@ -924,19 +926,21 @@
             if chunk:
                 gathered(far, chunk - 1)
                 project(far, chunk - 1)
+            if chunk == chunks - 2:
+                relay_out(1, o_first[1:], True)
             if chunk == 1:
                 relay_out(1, None, False)
             if chunk == chunks - 1:
-                relay_out(1, o_first, True)
-                crossed(far, chunks - 1)
                 for ready in range(chunks - 2):
                     temporal(ready)
                     settle(ready)
-                relay_out(1, o_last, True)
-        for ready in (chunks - 2, chunks - 1):
-            temporal(ready)
-            settle(ready)
+                    relay_out(1, o_last[ready : ready + 1], True)
+                crossed(far, chunks - 1)
+        temporal(chunks - 2)
+        settle(chunks - 2)
         relay_out(2, o_first, True)
+        temporal(chunks - 1)
+        settle(chunks - 1)
         spatial(far)
         for chunk in range(chunks):
             send(far, chunk)
@@ -980,30 +984,23 @@
 
     @pl.when(ended)
     def _():
-        relay_end(2, None)
+        relay_end(2, o_first)
         for chunk in range(chunks):
             arrive(chunk, nearer)
-            if chunk:
-                pass_on(chunk - 1, nearer)
             if chunk == chunks // 2 - 1:
+                relay_end(2, o_last)
                 relay_end(3, o_first)
-        pass_on(chunks - 1, nearer)
-
-    @pl.when(seated)
-    def _():
-        for chunk in range(chunks):
-            pass_on(chunk, nearer)
 
     for chunk in range(chunks):
         arrive(chunk, farther)
-        if chunk:
-            pass_on(chunk - 1, farther)
-        if chunk < len(o_last):
+        if chunk % 2:
             @pl.when(ended)
             def _():
-                relay_end(3, o_last[chunk : chunk + 1])
-
-    pass_on(chunks - 1, farther)
+                relay_end(3, o_last[chunk // 2 :: chunks // 2])
+
+    for seat in (nearer, farther):
+        for chunk in range(chunks):
+            pass_on(chunk, seat)
 
     @pl.when(seated)
     def _():
@@ -1129,10 +1126,10 @@
     def present(self, step, way):
         return self.me >= step if way == 0 else self.me + step < self.count
 
-    def open_way(self, way):
+    def open_way(self, way, chunks=None):
         @pl.when(self.onward(way))
         def _():
-            for chunk in range(self.chunks):
+            for chunk in range(self.chunks) if chunks is None else chunks:
                 self.along(self.me, chunk, way).start()
 
     def relay(self, step, way, chunks=None):

time: 127 us -> 120 us (0.945)
  Pallas kernels: 124 us -> 118 us
    pallas_call x1, Pallas kernels: 124 us -> 118 us  [by_pair(): pl.pallas_call(functools.partial(by_pair_kernel, sizes, chunks, pieces, o...]
where the time goes in v3:
time: 120 us
  Pallas kernels  118 us (98%)
  local copies, waits for them, and re-layouts  2.06 us (2%)
    pallas_call x1, Pallas kernels, by_pair(): pl.pallas_call(functools.partial(by_pair_kernel, sizes, chunks, pieces, o...  118 us

profile of v3, /device:TPU:0, one launch (start us, length us, event | category | flops | bytes accessed | tf_op | source)
XLA Modules:
  0.0 120.0 jit_solution(10932428916181412251)
XLA Ops:
  0.0 117.9 %by_pair.1 = bf16[512,768]{1,0:T(8,128)(2,1)} custom-call(bf16[512,3072]{1,0:T(8,128)(2,1)} %tokens.1, f32[3,3072]{1,0:T(4,128)} %modulation.1, bf16[768,2,768]{2,1,0:T(2,128)(2,1)} %w_own.1, bf16[512,768]{1,0:T(8,128)(2,1)} %o_own.1, s32[4,4]{1,0:T(4,128)} %pattern.1, s32[1,4]{1,0:T(1,128)} %bitcast.3, s32[4,4]{1,0:T(4,128)} %bitcast.2), custom_call_target="tpu_custom_call" | custom-call | tf_op jit(solution)/shard_map/by_pair/pallas_call | solution.py:1191
  117.9 2.1 %copy.9 = bf16[512,768]{1,0:T(8,128)(2,1)} copy(bf16[512,768]{1,0:T(8,128)(2,1)} %by_pair.1) | data formatting | bytes 1572864

commit v4 on v3

--- a/solution.py
+++ b/solution.py
@@ -790,6 +790,11 @@
         crossed_w(other)
         all_in(me)
         first_part(me, 0)
+        for source in (near, other, far):
+            l_push_from(lists_all, lists, l_sems, source, low, me).wait_recv()
+        keep.wait()
+        to_table = pltpu.make_async_copy(lists_all, table, own_sems.at[3])
+        to_table.start()
         for i in range(rest):
             if i + 1 < chunks:
                 land(other, i + 1)
@@ -800,18 +805,6 @@
             if i == rest - 1:
                 all_in(near)
                 first_part(near, 1)
-        for i in range(1, chunks):
-            crossed(other, i)
-        land(far, 0)
-        all_in(other)
-        first_part(other, 2)
-
-        for source in (near, other, far):
-            l_push_from(lists_all, lists, l_sems, source, low, me).wait_recv()
-        keep.wait()
-        to_table = pltpu.make_async_copy(lists_all, table, own_sems.at[3])
-        to_table.start()
-
         def project(frame, chunk):
             rows = pl.ds(pl.multiple_of(chunk * block, block), block)
             total = jnp.dot(
@@ -819,15 +812,26 @@
             ).astype(tq.dtype)
             keep_qkv(frame, chunk, total)
 
+        def add_part(frame, slot, source):
+            at = pl.ds(pl.multiple_of(source * depth, depth), depth)
+
+            def some_rows(chunk, carry):
+                rows = pl.ds(pl.multiple_of(chunk * block, block), block)
+                partial[slot, rows, :] += jnp.dot(
+                    hfull[frame, rows, at], wfull[source], preferred_element_type=jnp.float32
+                )
+                return carry
+
+            lax.fori_loop(0, chunks, some_rows, 0)
+
         def project_frame(frame, slot):
+            at = pl.ds(pl.multiple_of(near * depth, depth), depth)
+
             def last_part(chunk, carry):
                 rows = pl.ds(pl.multiple_of(chunk * block, block), block)
-                total = partial[slot, rows, :]
-                for source in (0, count - 1):
-                    at = slice(source * depth, (source + 1) * depth)
-                    total = total + jnp.dot(
-                        hfull[frame, rows, at], wfull[source], preferred_element_type=jnp.float32
-                    )
+                total = partial[slot, rows, :] + jnp.dot(
+                    hfull[frame, rows, at], wfull[near], preferred_element_type=jnp.float32
+                )
                 keep_qkv(frame, chunk, total.astype(tq.dtype))
                 return carry
 
@@ -907,44 +911,60 @@
             for turn in range(1, subs):
                 to_sub(0, turn, me, chunk, mine).start()
 
-        early = (me, near, other)
-        for chunk in range(chunks + 1):
-            if 0 < chunk < chunks:
-                land(far, chunk)
-            if chunk and chunk < chunks:
-                crossed(far, chunk - 1)
-            if chunk == chunks - 2:
-                relay_out(1, o_first[:1], True)
-            if chunk == 0:
-                crossed_w(far)
-                crossed_w(near)
-                to_table.wait()
-            if chunk < len(early):
-                project_frame(early[chunk], chunk)
-            if chunk and chunk <= len(early):
-                spatial(early[chunk - 1])
-            if chunk:
-                gathered(far, chunk - 1)
-                project(far, chunk - 1)
-            if chunk == chunks - 2:
-                relay_out(1, o_first[1:], True)
-            if chunk == 1:
-                relay_out(1, None, False)
-            if chunk == chunks - 1:
-                for ready in range(chunks - 2):
-                    temporal(ready)
-                    settle(ready)
-                    relay_out(1, o_last[ready : ready + 1], True)
-                crossed(far, chunks - 1)
-        temporal(chunks - 2)
-        settle(chunks - 2)
-        relay_out(2, o_first, True)
-        temporal(chunks - 1)
-        settle(chunks - 1)
+        def far_project(chunk):
+            gathered(far, chunk)
+            project(far, chunk)
+
+        crossed(other, 1)
+        land(far, 0)
+        crossed_w(far)
+        add_part(me, 0, far)
+        crossed(other, 2)
+        add_part(near, 1, far)
+        crossed(other, 3)
+        land(far, 1)
+        all_in(other)
+        first_part(other, 2)
+        add_part(other, 2, far)
+        crossed_w(near)
+        to_table.wait()
+        project_frame(me, 0)
+        land(far, 2)
+        crossed(far, 0)
+        project_frame(near, 1)
+        project_frame(other, 2)
+        relay_out(1, None, False)
+        land(far, 3)
+        crossed(far, 1)
+        far_project(0)
+        far_project(1)
+        spatial(me)
+        relay_out(1, (0,), True)
+        spatial(near)
+        spatial(other)
+        temporal(0)
+        settle(0)
+        crossed(far, 2)
+        relay_out(1, (1,), True)
+        far_project(2)
+        temporal(1)
+        settle(1)
+        relay_out(1, (2,), True)
+        crossed(far, 3)
+        relay_out(1, (3,), True)
+        far_project(3)
         spatial(far)
-        for chunk in range(chunks):
-            send(far, chunk)
-        relay_out(2, o_last, True)
+        send(far, 0)
+        send(far, 1)
+        relay_out(2, (0,), True)
+        temporal(2)
+        settle(2)
+        send(far, 2)
+        relay_out(2, (1,), True)
+        temporal(3)
+        settle(3)
+        send(far, 3)
+        relay_out(2, (2, 3), True)
 
     def arrive(chunk, seat):
         out_push(own, slots, sz_sems, seat, me, chunk, block, low).wait_recv()
@@ -962,19 +982,30 @@
     columns = pl.ds(pl.multiple_of((head * subs + sub) * update.shape[1], 128), update.shape[1])
     gate = modulation[2:3, columns]
 
-    def finish(chunk):
-        for seat in (low, high):
-            for hop in range(heads):
-                for turn in range(1, subs):
-                    to_sub(hop, turn, seat, chunk).wait_recv()
-        rows = slice(chunk * block, (chunk + 1) * block)
-        total = None
-        for hop in range(heads):
-            for turn in range(subs):
-                owner = lax.rem(head + heads - hop, heads) * subs + lax.rem(sub + subs - turn, subs)
-                product = jnp.dot(slots[hop, turn, rows, :], o_all[owner], preferred_element_type=jnp.float32)
-                total = product if total is None else total + product
-        update[rows, :] = (gate * total).astype(update.dtype)
+    def product(shard, chunk):
+        hop = lax.rem(head + heads - shard // subs, heads)
+        turn = lax.rem(sub + subs - lax.rem(shard, subs), subs)
+        rows = pl.ds(pl.multiple_of(chunk * block, block), block)
+        return rows, jnp.dot(slots[hop, turn, rows, :], o_all[shard], preferred_element_type=jnp.float32)
+
+    def gather_up(shards):
+        def some_rows(chunk, carry):
+            total = None
+            for shard in shards:
+                rows, term = product(shard, chunk)
+                total = term if total is None else total + term
+            partial[0, rows, :] = total
+            return carry
+
+        lax.fori_loop(0, chunks, some_rows, 0)
+
+    def finish(shard):
+        def some_rows(chunk, carry):
+            rows, term = product(shard, chunk)
+            update[rows, :] = (gate * (partial[0, rows, :] + term)).astype(update.dtype)
+            return carry
+
+        lax.fori_loop(0, chunks, some_rows, 0)
 
     nearer = jnp.where(seated, me, toward)
     farther = low + high - nearer
@@ -998,22 +1029,28 @@
             def _():
                 relay_end(3, o_last[chunk // 2 :: chunks // 2])
 
-    for seat in (nearer, farther):
-        for chunk in range(chunks):
-            pass_on(chunk, seat)
+    for chunk in range(chunks):
+        pass_on(chunk, nearer)
 
     @pl.when(seated)
     def _():
         for chunk in range(chunks):
             keep_out(own, slots, keep_sems, me, chunk, block, low).wait()
 
-    for step in range(1, count):
-        for way in (0, 1):
-            @pl.when(outs.present(step, way))
-            def _():
-                outs.complete(outs.shard_of(step, way))
     for chunk in range(chunks):
-        finish(chunk)
+        pass_on(chunk, farther)
+    last = jnp.where(ended, count - 1 - me, far)
+    middle = (jnp.where(ended, toward, near), jnp.where(ended, low + high - toward, other))
+    for shard in middle:
+        outs.complete(shard)
+    for chunk in range(chunks):
+        for seat in (nearer, farther):
+            for hop in range(heads):
+                for turn in range(1, subs):
+                    to_sub(hop, turn, seat, chunk).wait_recv()
+    gather_up((me,) + middle)
+    outs.complete(last)
+    finish(last)
 
     for seat in (low, high):
         @pl.when(me != seat)
@@ -1241,7 +1278,7 @@
         and w_qkv.shape[1] == len(seats(count))
         and frames == 1
         and rows == BLOCK * pattern.shape[0] == BLOCK * spatial_mask.shape[1]
-        and pattern.shape[0] < 8
+        and pattern.shape[0] == count
         and BLOCK % (16 * count) == 0
         and w_qkv.shape[0] % (192 * parts) == 0
         and w_out.shape[0] % (64 * parts) == 0

time: 120 us -> 120 us (level)
  no operation moved by 1% of the time
where the time goes in v4:
time: 120 us; the launch traced here: 119 us
  Pallas kernels  117 us (98%)
  local copies, waits for them, and re-layouts  2.06 us (2%)
    pallas_call x1, Pallas kernels, by_pair(): pl.pallas_call(functools.partial(by_pair_kernel, sizes, chunks, pieces, o...  117 us

profile of v4, /device:TPU:0, one launch (start us, length us, event | category | flops | bytes accessed | tf_op | source)
XLA Modules:
  0.0 119.3 jit_solution(16964269887568528654)
XLA Ops:
  0.0 117.2 %by_pair.1 = bf16[512,768]{1,0:T(8,128)(2,1)} custom-call(bf16[512,3072]{1,0:T(8,128)(2,1)} %tokens.1, f32[3,3072]{1,0:T(4,128)} %modulation.1, bf16[768,2,768]{2,1,0:T(2,128)(2,1)} %w_own.1, bf16[512,768]{1,0:T(8,128)(2,1)} %o_own.1, s32[4,4]{1,0:T(4,128)} %pattern.1, s32[1,4]{1,0:T(1,128)} %bitcast.3, s32[4,4]{1,0:T(4,128)} %bitcast.2), custom_call_target="tpu_custom_call" | custom-call | tf_op jit(solution)/shard_map/by_pair/pallas_call | solution.py:1228
  117.2 2.1 %copy.9 = bf16[512,768]{1,0:T(8,128)(2,1)} copy(bf16[512,768]{1,0:T(8,128)(2,1)} %by_pair.1) | data formatting | bytes 1572864

commit v5 on v4

--- a/solution.py
+++ b/solution.py
@@ -465,8 +465,9 @@
 def by_pair_kernel(
     sizes, chunks, pieces, o_chunks,
     tokens, modulation, w_own, o_own, pattern, counts, mask, update,
-    held, raw, stage, passing, partial, hfull, wfull, tq, sq, o_all, lists, lists_all, table, own, slots,
-    tok_sems, l_sems, w_sems, p_sems, z_sems, x_sems, c_sems, o_sems, keep_sems, sz_sems, sx_sems, sc_sems, own_sems,
+    held, raw, stage, passing, partial, hfull, wfull, tq, sq, o_all, lists, lists_all, table, own, slots, result,
+    tok_sems, l_sems, w_sems, wa_sems, p_sems, z_sems, x_sems, c_sems, o_sems, oa_sems,
+    sz_sems, sx_sems, sc_sems, own_sems, sent,
 ):
     count, parts, heads, subs = sizes
     low, high = seats(count)
@@ -502,8 +503,18 @@
     def fetch(hop, chunk):
         return pltpu.make_async_copy(
             tokens.at[rows_of(hop, 0, chunk)], held.at[hop, pl.ds(chunk * unit, unit)],
-            tok_sems.at[hop, chunk],
-        )
+            tok_sems.at[hop, min(chunk, 1) if hop == 0 else 0],
+        )
+
+    def fetched(hop, first, last):
+        pltpu.make_async_copy(
+            tokens.at[pl.ds(first * unit, (last - first) * unit)],
+            held.at[hop, pl.ds(first * unit, (last - first) * unit)],
+            tok_sems.at[hop, min(first, 1) if hop == 0 else 0],
+        ).wait()
+
+    def taken(region, sem):
+        push(region, region, sem, sem, "seq", me).wait_recv()
 
     for chunk in range(chunks):
         fetch(0, chunk).start()
@@ -539,8 +550,7 @@
             hfull[me, pl.ds(pl.multiple_of(start, 16), 16), :] = (normed * gain + shift).astype(hfull.dtype)
             return carry
 
-        for chunk in range(first, last):
-            fetch(hop, chunk).wait()
+        fetched(hop, first, last)
         lax.fori_loop(first * unit // 16, last * unit // 16, some, 0, unroll=2)
 
     modulate_rows(0, 0, 1)
@@ -551,24 +561,24 @@
 
     def z_push(frame, chunk, place):
         target = spot(frame, 0, 0, chunk)
-        return push(target, target, z_sems.at[0, frame, chunk], z_sems.at[1, frame, chunk], "seq", place)
+        return push(target, target, sent.at[1], z_sems.at[frame, chunk], "seq", place)
 
     def x_push(frame, chunk, hop):
         target = spot(frame, 0, 0, chunk)
         return push(
-            target, target, x_sems.at[hop, 0, frame, chunk], x_sems.at[hop, 1, frame, chunk],
+            target, target, sent.at[2], x_sems.at[frame, chunk],
             "head", lax.rem(head + hop, heads),
         )
 
     def c_push(frame, chunk, hop, turn):
         target = spot(frame, hop, 0, chunk)
         return push(
-            target, target, c_sems.at[hop, turn, 0, frame, chunk], c_sems.at[hop, turn, 1, frame, chunk],
+            target, target, sent.at[3], c_sems.at[frame, chunk],
             "sub", lax.rem(sub + turn, subs),
         )
 
     def l_push(seat):
-        return push(lists, lists_all.at[me], l_sems.at[0, seat - low], l_sems.at[1, me], "seq", seat)
+        return push(lists, lists_all.at[me], sent.at[9], l_sems.at[me], "seq", seat)
 
     def w_rows(part, step):
         return pl.ds(pl.multiple_of(part * half + step * piece, piece), piece)
@@ -576,30 +586,30 @@
     def w_along(seat, source, step):
         return push(
             stage.at[seat - low, pl.ds(step * piece, piece)], wfull.at[source, w_rows(group, step)],
-            w_sems.at[0, 0, seat - low, step], w_sems.at[0, 1, source, step], "seq", seat,
+            sent.at[0], w_sems.at[source, step], "seq", seat,
         )
 
     def w_hand(step, place):
         return push(
             stage.at[jnp.where(me < low, high, low) - low, pl.ds(step * piece, piece)],
             passing.at[pl.ds(step * piece, piece)],
-            p_sems.at[0, step], p_sems.at[1, step], "seq", place,
+            sent.at[0], p_sems.at[step], "seq", place,
         )
 
     def w_pass(source, step):
         return push(
             passing.at[pl.ds(step * piece, piece)], wfull.at[source, w_rows(group, step)],
-            w_sems.at[0, 0, me - low, step], w_sems.at[0, 1, source, step], "seq", other,
+            sent.at[0], w_sems.at[source, step], "seq", other,
         )
 
     def w_across(source, step, turn):
         target = wfull.at[source, w_rows(group, step)]
         return push(
-            target, target, w_sems.at[turn, 0, source, step], w_sems.at[turn, 1, source, step],
+            target, target, sent.at[4], wa_sems.at[source],
             "groups", lax.rem(group + turn, parts),
         )
 
-    outs = LineGather(o_all, o_sems, o_chunks, count, parts)
+    outs = LineGather(o_all, o_sems, oa_sems, sent, o_chunks, count, parts)
 
     for seat in (low, high):
         @pl.when(me != seat)
@@ -614,14 +624,14 @@
     def to_head(hop, seat, chunk, source=None):
         return push(
             item(0, 0, seat, chunk) if source is None else source, item(hop, 0, seat, chunk),
-            sx_sems.at[hop, 0, seat - low, chunk], sx_sems.at[hop, 1, seat - low, chunk],
+            sent.at[7], sx_sems.at[seat - low, chunk],
             "head", lax.rem(head + hop, heads),
         )
 
     def to_sub(hop, turn, seat, chunk, source=None):
         return push(
             item(hop, 0, seat, chunk) if source is None else source, item(hop, turn, seat, chunk),
-            sc_sems.at[hop, turn, 0, seat - low, chunk], sc_sems.at[hop, turn, 1, seat - low, chunk],
+            sent.at[8], sc_sems.at[chunk],
             "sub", lax.rem(sub + turn, subs),
         )
 
@@ -714,9 +724,7 @@
                     c_push(frame, chunk, hop, turn).start()
 
         def gathered(frame, chunk):
-            for hop in range(heads):
-                for turn in range(1, subs):
-                    c_push(frame, chunk, hop, turn).wait_recv()
+            taken(hfull.at[frame, pl.ds(0, heads * (subs - 1) * unit)], c_sems.at[frame, chunk])
 
         def keep_pair(i, carry):
             at = pl.ds(pl.multiple_of(i * 64, 64), 64)
@@ -747,7 +755,7 @@
                 )
                 return carry
 
-            lax.fori_loop(0, chunks, some_rows, 0)
+            lax.fori_loop(0, chunks, some_rows, 0, unroll=2)
 
         def keep_qkv(frame, chunk, total):
             at = pl.ds(pl.multiple_of(frame * span, span), span)
@@ -779,9 +787,7 @@
             def _():
                 outs.open_way(way)
         def crossed_w(source):
-            for step in range(pieces):
-                for turn in range(1, parts):
-                    w_across(source, step, turn).wait_recv()
+            taken(wfull.at[source, pl.ds(0, (parts - 1) * half)], wa_sems.at[source])
 
         def all_in(frame):
             for chunk in range(chunks):
@@ -791,7 +797,7 @@
         all_in(me)
         first_part(me, 0)
         for source in (near, other, far):
-            l_push_from(lists_all, lists, l_sems, source, low, me).wait_recv()
+            taken(lists, l_sems.at[source])
         keep.wait()
         to_table = pltpu.make_async_copy(lists_all, table, own_sems.at[3])
         to_table.start()
@@ -822,7 +828,7 @@
                 )
                 return carry
 
-            lax.fori_loop(0, chunks, some_rows, 0)
+            lax.fori_loop(0, chunks, some_rows, 0, unroll=2)
 
         def project_frame(frame, slot):
             at = pl.ds(pl.multiple_of(near * depth, depth), depth)
@@ -835,7 +841,7 @@
                 keep_qkv(frame, chunk, total.astype(tq.dtype))
                 return carry
 
-            lax.fori_loop(0, chunks, last_part, 0)
+            lax.fori_loop(0, chunks, last_part, 0, unroll=2)
 
         def soft(q, keys, values, biases):
             scores = lax.dot_general(
@@ -880,7 +886,7 @@
                     own[f, at, :size] = result[f * span : (f + 1) * span]
                 return carry
 
-            lax.fori_loop(0, blocks, query, 0)
+            lax.fori_loop(0, blocks, query, 0, unroll=True)
 
         def spatial(frame):
             per = sq.shape[1] // BLOCK
@@ -896,15 +902,15 @@
                 )
                 return carry
 
-            lax.fori_loop(0, per, query, 0)
+            lax.fori_loop(0, per, query, 0, unroll=True)
 
         def send(frame, chunk):
-            out_push(own, slots, sz_sems, me, frame, chunk, block, low).start()
+            out_push(own, slots, sz_sems, sent, me, frame, chunk, block, low).start()
 
         def settle(chunk):
             send(near, chunk)
             send(other, chunk)
-            keep_out(own, slots, keep_sems, me, chunk, block, low).start()
+            keep_out(own, slots, own_sems.at[4], me, chunk, block, low).start()
             mine = own.at[me, pl.ds(chunk * block, block)]
             for hop in range(1, heads):
                 to_head(hop, me, chunk, mine).start()
@@ -967,7 +973,7 @@
         relay_out(2, (2, 3), True)
 
     def arrive(chunk, seat):
-        out_push(own, slots, sz_sems, seat, me, chunk, block, low).wait_recv()
+        out_push(own, slots, sz_sems, sent, seat, me, chunk, block, low).wait_recv()
         for hop in range(1, heads):
             to_head(hop, seat, chunk).start()
         for turn in range(1, subs):
@@ -979,33 +985,31 @@
             for turn in range(1, subs):
                 to_sub(hop, turn, seat, chunk).start()
 
+    o_half = o_all.shape[1] // parts
     columns = pl.ds(pl.multiple_of((head * subs + sub) * update.shape[1], 128), update.shape[1])
     gate = modulation[2:3, columns]
 
     def product(shard, chunk):
         hop = lax.rem(head + heads - shard // subs, heads)
         turn = lax.rem(sub + subs - lax.rem(shard, subs), subs)
-        rows = pl.ds(pl.multiple_of(chunk * block, block), block)
+        rows = pl.ds(chunk * block, block)
         return rows, jnp.dot(slots[hop, turn, rows, :], o_all[shard], preferred_element_type=jnp.float32)
 
-    def gather_up(shards):
-        def some_rows(chunk, carry):
-            total = None
-            for shard in shards:
-                rows, term = product(shard, chunk)
-                total = term if total is None else total + term
-            partial[0, rows, :] = total
-            return carry
-
-        lax.fori_loop(0, chunks, some_rows, 0)
-
-    def finish(shard):
-        def some_rows(chunk, carry):
+    def gather_up(shards, chunk):
+        total = None
+        for shard in shards:
             rows, term = product(shard, chunk)
-            update[rows, :] = (gate * (partial[0, rows, :] + term)).astype(update.dtype)
-            return carry
-
-        lax.fori_loop(0, chunks, some_rows, 0)
+            total = term if total is None else total + term
+        partial[0, rows, :] = total
+
+    def put(chunk):
+        rows = pl.ds(chunk * block, block)
+        return pltpu.make_async_copy(result.at[rows], update.at[rows], own_sems.at[5])
+
+    def finish(shard, chunk):
+        rows, term = product(shard, chunk)
+        result[rows, :] = (gate * (partial[0, rows, :] + term)).astype(result.dtype)
+        put(chunk).start()
 
     nearer = jnp.where(seated, me, toward)
     farther = low + high - nearer
@@ -1034,74 +1038,49 @@
 
     @pl.when(seated)
     def _():
-        for chunk in range(chunks):
-            keep_out(own, slots, keep_sems, me, chunk, block, low).wait()
-
-    for chunk in range(chunks):
-        pass_on(chunk, farther)
+        pltpu.make_async_copy(own.at[0], own.at[0], own_sems.at[4]).wait()
+
     last = jnp.where(ended, count - 1 - me, far)
     middle = (jnp.where(ended, toward, near), jnp.where(ended, low + high - toward, other))
     for shard in middle:
         outs.complete(shard)
+
+    def add_up(chunk):
+        taken(slots.at[pl.ds(0, heads), 0, pl.ds(0, block)], sc_sems.at[chunk])
+        gather_up((me,) + middle, chunk)
+
     for chunk in range(chunks):
-        for seat in (nearer, farther):
-            for hop in range(heads):
-                for turn in range(1, subs):
-                    to_sub(hop, turn, seat, chunk).wait_recv()
-    gather_up((me,) + middle)
+        pass_on(chunk, farther)
+        if chunk:
+            add_up(chunk - 1)
     outs.complete(last)
-    finish(last)
-
-    for seat in (low, high):
-        @pl.when(me != seat)
-        def _():
-            l_push(seat).wait_send()
+    for chunk in range(chunks - 1):
+        finish(last, chunk)
+    add_up(chunks - 1)
+    finish(last, chunks - 1)
+
+    taken(stage, sent.at[0])
+    taken(slots.at[0, 0], sent.at[7])
+    taken(slots.at[0], sent.at[8])
+    taken(o_all.at[pl.ds(0, count - 1), pl.ds(0, (parts - 1) * o_half)], sent.at[10])
 
     @pl.when(ended)
     def _():
-        for step in range(pieces):
-            w_hand(step, toward).wait_send()
-            w_along(toward, me, step).wait_send()
-        for chunk in range(chunks):
-            z_push(me, chunk, jnp.where(me < low, low, high)).wait_send()
+        taken(hfull.at[0, pl.ds(0, quarter)], sent.at[1])
+        taken(lists_all.at[pl.ds(0, 2)], sent.at[9])
+        taken(o_all.at[0, pl.ds(0, o_half)], sent.at[5])
 
     @pl.when(seated)
     def _():
-        for step in range(pieces):
-            w_along(other, me, step).wait_send()
-            w_pass(near, step).wait_send()
-        for chunk in range(chunks):
-            z_push(me, chunk, other).wait_send()
-            z_push(near, chunk, other).wait_send()
-            for frame in (me, near, other, far):
-                for hop in range(heads):
-                    for turn in range(1, subs):
-                        c_push(frame, chunk, hop, turn).wait_send()
-            for frame in (near, other, far):
-                for hop in range(1, heads):
-                    x_push(frame, chunk, hop).wait_send()
-                out_push(own, slots, sz_sems, me, frame, chunk, block, low).wait_send()
-        for source in (near, other, far):
-            for step in range(pieces):
-                for turn in range(1, parts):
-                    w_across(source, step, turn).wait_send()
-
-    for way in (0, 1):
-        outs.close_way(way)
-    for step in range(1, count):
-        for way in (0, 1):
-            outs.close_sends(step, way)
-    for chunk in range(chunks):
-        for seat in (low, high):
-            for hop in range(1, heads):
-                to_head(hop, seat, chunk).wait_send()
-            for hop in range(heads):
-                for turn in range(1, subs):
-                    to_sub(hop, turn, seat, chunk).wait_send()
-
-
-def l_push_from(lists_all, lists, l_sems, source, low, me):
-    return push(lists, lists_all.at[source], l_sems.at[0, me - low], l_sems.at[1, source], "seq", me)
+        taken(hfull.at[0, pl.ds(0, 2 * quarter)], sent.at[1])
+        taken(lists, sent.at[9])
+        taken(hfull.at[0, pl.ds(0, (count - 1) * quarter)], sent.at[2])
+        taken(hfull.at[pl.ds(0, 2)], sent.at[3])
+        taken(wfull.at[pl.ds(0, count - 1), pl.ds(0, half)], sent.at[4])
+        taken(o_all.at[pl.ds(0, count), pl.ds(0, 5 * o_half // count)], sent.at[5])
+        taken(own.at[pl.ds(0, count - 1)], sent.at[6])
+
+    pltpu.make_async_copy(result, update, own_sems.at[5]).wait()
 
 
 def out_spot(slots, hop, turn, seat, chunk, block, low, columns):
@@ -1110,26 +1089,27 @@
     return slots.at[hop, turn, pl.ds(chunk * block, block), at]
 
 
-def out_push(own, slots, sems, seat, frame, chunk, block, low):
+def out_push(own, slots, sems, sent, seat, frame, chunk, block, low):
     return push(
         own.at[frame, pl.ds(chunk * block, block)],
         out_spot(slots, 0, 0, seat, chunk, block, low, own.shape[2]),
-        sems.at[0, frame, chunk], sems.at[1, seat, chunk], "seq", frame,
+        sent.at[6], sems.at[seat - low, chunk], "seq", frame,
     )
 
 
-def keep_out(own, slots, sems, seat, chunk, block, low):
+def keep_out(own, slots, sem, seat, chunk, block, low):
     return pltpu.make_async_copy(
         own.at[seat, pl.ds(chunk * block, block)],
         out_spot(slots, 0, 0, seat, chunk, block, low, own.shape[2]),
-        sems.at[chunk],
+        sem,
     )
 
 
 class LineGather:
-    def __init__(self, slots, sems, chunks, count, parts):
+    def __init__(self, slots, sems, across_sems, sent, chunks, count, parts):
         self.slots, self.chunks = slots, chunks
-        self.sems, self.count, self.parts = sems, count, parts
+        self.sems, self.across_sems, self.sent = sems, across_sems, sent
+        self.count, self.parts = count, parts
         self.me = lax.axis_index("seq")
         self.group = lax.axis_index("groups")
         self.size = slots.shape[1] // (parts * chunks)
@@ -1142,7 +1122,7 @@
         rows = self.rows(self.group, chunk)
         return push(
             self.slots.at[shard, rows], self.slots.at[shard, rows],
-            self.sems.at[way, 0, shard, chunk], self.sems.at[way, 1, shard, chunk],
+            self.sent.at[5], self.sems.at[shard, chunk],
             "seq", self.me + (1 if way == 0 else -1),
         )
 
@@ -1150,7 +1130,7 @@
         rows = self.rows(self.group, chunk)
         return push(
             self.slots.at[shard, rows], self.slots.at[shard, rows],
-            self.sems.at[1 + hop, 0, shard, chunk], self.sems.at[1 + hop, 1, shard, chunk],
+            self.sent.at[10], self.across_sems.at[shard],
             "groups", lax.rem(self.group + hop, self.parts),
         )
 
@@ -1163,10 +1143,10 @@
     def present(self, step, way):
         return self.me >= step if way == 0 else self.me + step < self.count
 
-    def open_way(self, way, chunks=None):
+    def open_way(self, way):
         @pl.when(self.onward(way))
         def _():
-            for chunk in range(self.chunks) if chunks is None else chunks:
+            for chunk in range(self.chunks):
                 self.along(self.me, chunk, way).start()
 
     def relay(self, step, way, chunks=None):
@@ -1185,28 +1165,9 @@
                     self.across(shard, chunk, hop).start()
 
     def complete(self, shard):
-        for chunk in range(self.chunks):
-            for hop in range(1, self.parts):
-                self.across(shard, chunk, hop).wait_recv()
-
-    def close_sends(self, step, way):
-        shard = self.shard_of(step, way)
-
-        @pl.when(self.present(step, way))
-        def _():
-            for chunk in range(self.chunks):
-                @pl.when(self.onward(way))
-                def _():
-                    self.along(shard, chunk, way).wait_send()
-
-                for hop in range(1, self.parts):
-                    self.across(shard, chunk, hop).wait_send()
-
-    def close_way(self, way):
-        @pl.when(self.onward(way))
-        def _():
-            for chunk in range(self.chunks):
-                self.along(self.me, chunk, way).wait_send()
+        region = self.slots.at[shard, pl.ds(0, (self.parts - 1) * self.chunks * self.size)]
+        sem = self.across_sems.at[shard]
+        push(region, region, sem, sem, "seq", self.me).wait_recv()
 
 
 def by_pair(tokens, modulation, w_own, o_own, pattern, counts, mask):
@@ -1229,7 +1190,7 @@
         functools.partial(by_pair_kernel, sizes, chunks, pieces, o_chunks),
         out_shape=jax.ShapeDtypeStruct((rows, o_own.shape[1]), kept),
         in_specs=[whole, vmem, whole, whole, vmem, vmem, vmem],
-        out_specs=vmem,
+        out_specs=whole,
         scratch_shapes=[
             pltpu.VMEM((heads, quarter, depth), kept),
             pltpu.VMEM(w_own.shape, kept),
@@ -1246,19 +1207,22 @@
             pltpu.SMEM((count, 24, 128), jnp.int32),
             pltpu.VMEM((count, rows, columns), kept),
             pltpu.VMEM((heads, subs, rows, seated * columns), kept),
-            dma((heads, chunks)),
-            dma((2, count)),
-            dma((parts, 2, count, pieces)),
-            dma((2, pieces)),
-            dma((2, count, chunks)),
-            dma((heads, 2, count, chunks)),
-            dma((heads, subs, 2, count, chunks)),
-            dma((1 + parts, 2, count, o_chunks)),
+            pltpu.VMEM((rows, o_own.shape[1]), kept),
+            dma((heads, 2)),
+            dma((count,)),
+            dma((count, pieces)),
+            dma((count,)),
+            dma((pieces,)),
+            dma((count, chunks)),
+            dma((count, chunks)),
+            dma((count, chunks)),
+            dma((count, o_chunks)),
+            dma((count,)),
+            dma((seated, chunks)),
+            dma((seated, chunks)),
             dma((chunks,)),
-            dma((2, count, chunks)),
-            dma((heads, 2, seated, chunks)),
-            dma((heads, subs, 2, seated, chunks)),
-            dma((4,)),
+            dma((6,)),
+            dma((11,)),
         ],
         compiler_params=pltpu.CompilerParams(
             collective_id=2, has_side_effects=True, vmem_limit_bytes=60 * 1024 * 1024
@@ -1271,10 +1235,11 @@
     return by_pair(tokens, modulation, w_qkv, w_out, pattern, counts[None, :], spatial_mask[0])
 
 
-def one_pair_each(count, blocks, parts, tokens, w_qkv, w_out, pattern, spatial_mask):
+def one_pair_each(count, heads, subs, parts, tokens, w_qkv, w_out, pattern, spatial_mask):
     rows, frames = tokens.shape[0], spatial_mask.shape[0]
     return (
-        count == blocks == 4
+        count == 4
+        and heads == subs == parts == 2
         and w_qkv.shape[1] == len(seats(count))
         and frames == 1
         and rows == BLOCK * pattern.shape[0] == BLOCK * spatial_mask.shape[1]
@@ -1287,8 +1252,7 @@
 
 def shards_any(*args):
     tokens, _, w_qkv, w_out, pattern, _, spatial_mask = args
-    blocks = lax.axis_size("head") * lax.axis_size("sub")
-    sizes = lax.axis_size("seq"), blocks, lax.axis_size("groups")
+    sizes = tuple(lax.axis_size(axis) for axis in ("seq", "head", "sub", "groups"))
     if one_pair_each(*sizes, tokens, w_qkv, w_out, pattern, spatial_mask):
         return shards_by_pair(*args)
     return shards(*args)

time: 120 us -> 112 us (0.933)
  Pallas kernels: 117 us -> 110 us
    pallas_call x1, Pallas kernels: 117 us -> 110 us  [by_pair(): pl.pallas_call(functools.partial(by_pair_kernel, sizes, chunks, pieces, o...]
where the time goes in v5:
time: 112 us
  Pallas kernels  110 us (98%)
  local copies, waits for them, and re-layouts  2.06 us (2%)
    pallas_call x1, Pallas kernels, by_pair(): pl.pallas_call(functools.partial(by_pair_kernel, sizes, chunks, pieces, o...  110 us

profile of v5, /device:TPU:0, one launch (start us, length us, event | category | flops | bytes accessed | tf_op | source)
XLA Modules:
  0.0 111.8 jit_solution(9166739789869123623)
XLA Ops:
  0.0 109.7 %by_pair.1 = bf16[512,768]{1,0:T(8,128)(2,1)} custom-call(bf16[512,3072]{1,0:T(8,128)(2,1)} %tokens.1, f32[3,3072]{1,0:T(4,128)} %modulation.1, bf16[768,2,768]{2,1,0:T(2,128)(2,1)} %w_own.1, bf16[512,768]{1,0:T(8,128)(2,1)} %o_own.1, s32[4,4]{1,0:T(4,128)} %pattern.1, s32[1,4]{1,0:T(1,128)} %bitcast.3, s32[4,4]{1,0:T(4,128)} %bitcast.2), custom_call_target="tpu_custom_call" | custom-call | tf_op jit(solution)/shard_map/by_pair/pallas_call | solution.py:1189
  109.8 2.1 %copy.9 = bf16[512,768]{1,0:T(8,128)(2,1)} copy(bf16[512,768]{1,0:T(8,128)(2,1)} %by_pair.1) | data formatting | bytes 1572864

commit v6 on v5

--- a/solution.py
+++ b/solution.py
@@ -577,6 +577,19 @@
             "sub", lax.rem(sub + turn, subs),
         )
 
+    def z_half(frame, part, place):
+        start = ((chunks - 1) * blocks + head * subs + sub) * unit + part * (unit // 2)
+        target = hfull.at[frame, pl.ds(pl.multiple_of(start, unit // 2), unit // 2)]
+        return push(target, target, sent.at[1], z_sems.at[frame, chunks - 1 + part], "seq", place)
+
+    def x_half(frame, part):
+        start = ((chunks - 1) * blocks + head * subs + sub) * unit + part * (unit // 2)
+        target = hfull.at[frame, pl.ds(pl.multiple_of(start, unit // 2), unit // 2)]
+        return push(
+            target, target, sent.at[2], x_sems.at[frame, chunks - 1 + part],
+            "head", lax.rem(head + 1, heads),
+        )
+
     def l_push(seat):
         return push(lists, lists_all.at[me], sent.at[9], l_sems.at[me], "seq", seat)
 
@@ -631,11 +644,17 @@
     def to_sub(hop, turn, seat, chunk, source=None):
         return push(
             item(hop, 0, seat, chunk) if source is None else source, item(hop, turn, seat, chunk),
-            sent.at[8], sc_sems.at[chunk],
+            sent.at[8], sc_sems.at[seat - low, chunk],
             "sub", lax.rem(sub + turn, subs),
         )
 
     toward = jnp.where(me < low, low, high)
+
+    def open_inward(pieces_of_it):
+        for way in (0, 1):
+            @pl.when(outward != way)
+            def _():
+                outs.open_way(way, pieces_of_it)
 
     def relay_out(step, pieces_of_it, outgoing):
         for way in (0, 1):
@@ -779,13 +798,17 @@
         for i in range(rest):
             if i + 1 < chunks:
                 land(near, i + 1)
-                z_push(near, i + 1, other).start()
+                if i == 1:
+                    open_inward(o_first)
+                if i + 2 < chunks:
+                    z_push(near, i + 1, other).start()
+                else:
+                    for part in (0, 1):
+                        z_half(near, part, other).start()
             if i < pieces:
                 w_land(far, i)
-        for way in (0, 1):
-            @pl.when(outward != way)
-            def _():
-                outs.open_way(way)
+        open_inward(o_last)
+
         def crossed_w(source):
             taken(wfull.at[source, pl.ds(0, (parts - 1) * half)], wa_sems.at[source])
 
@@ -934,30 +957,37 @@
         add_part(other, 2, far)
         crossed_w(near)
         to_table.wait()
+        relay_out(1, (0,), True)
         project_frame(me, 0)
-        land(far, 2)
         crossed(far, 0)
         project_frame(near, 1)
+        relay_out(1, (1,), True)
         project_frame(other, 2)
+        crossed(far, 1)
+        spatial(me)
+        land(far, 2)
+        spatial(near)
         relay_out(1, None, False)
-        land(far, 3)
-        crossed(far, 1)
         far_project(0)
         far_project(1)
-        spatial(me)
-        relay_out(1, (0,), True)
-        spatial(near)
         spatial(other)
+        for part in (0, 1):
+            z_half(far, part, other).wait_recv()
+            x_half(far, part).start()
+        for turn in range(1, subs):
+            c_push(far, 3, 0, turn).start()
         temporal(0)
         settle(0)
+        relay_out(1, (2,), True)
         crossed(far, 2)
-        relay_out(1, (1,), True)
         far_project(2)
         temporal(1)
         settle(1)
-        relay_out(1, (2,), True)
-        crossed(far, 3)
         relay_out(1, (3,), True)
+        for part in (0, 1):
+            x_half(far, part).wait_recv()
+        for turn in range(1, subs):
+            c_push(far, 3, 1, turn).start()
         far_project(3)
         spatial(far)
         send(far, 0)
@@ -989,75 +1019,107 @@
     columns = pl.ds(pl.multiple_of((head * subs + sub) * update.shape[1], 128), update.shape[1])
     gate = modulation[2:3, columns]
 
-    def product(shard, chunk):
+    def product(shard, chunk, seat):
         hop = lax.rem(head + heads - shard // subs, heads)
         turn = lax.rem(sub + subs - lax.rem(shard, subs), subs)
-        rows = pl.ds(chunk * block, block)
-        return rows, jnp.dot(slots[hop, turn, rows, :], o_all[shard], preferred_element_type=jnp.float32)
-
-    def gather_up(shards, chunk):
-        total = None
+        start = pl.multiple_of((seat - low) * columns_of, columns_of)
+        at = pl.ds(start, columns_of)
+        return jnp.dot(
+            slots[hop, turn, pl.ds(chunk * block, block), at], o_all[shard, at, :],
+            preferred_element_type=jnp.float32,
+        )
+
+    def add_up(chunk, seat, shards, total=None):
         for shard in shards:
-            rows, term = product(shard, chunk)
+            term = product(shard, chunk, seat)
             total = term if total is None else total + term
-        partial[0, rows, :] = total
+        return total
+
+    def passed(chunk, seat):
+        taken(slots.at[0, 0, pl.ds(chunk * block, block)], sc_sems.at[seat - low, chunk])
 
     def put(chunk):
         rows = pl.ds(chunk * block, block)
         return pltpu.make_async_copy(result.at[rows], update.at[rows], own_sems.at[5])
 
-    def finish(shard, chunk):
-        rows, term = product(shard, chunk)
-        result[rows, :] = (gate * (partial[0, rows, :] + term)).astype(result.dtype)
-        put(chunk).start()
-
     nearer = jnp.where(seated, me, toward)
     farther = low + high - nearer
+    last = jnp.where(ended, count - 1 - me, far)
+    middle = (jnp.where(ended, toward, near), jnp.where(ended, low + high - toward, other))
+
     def relay_end(step, pieces_of_it):
         for way in (0, 1):
             outs.relay(step, way, pieces_of_it)
 
+    def first_half(chunk):
+        passed(chunk, nearer)
+        rows = pl.ds(chunk * block, block)
+        partial[0, rows, :] = add_up(chunk, nearer, (me,) + middle)
+
+    def second_half(chunk):
+        passed(chunk, farther)
+        rows = pl.ds(chunk * block, block)
+        partial[0, rows, :] = add_up(chunk, farther, (me,) + middle, partial[0, rows, :])
+
+    def finish(chunk):
+        rows = pl.ds(chunk * block, block)
+        total = add_up(chunk, nearer, (last,), partial[0, rows, :])
+        total = add_up(chunk, farther, (last,), total)
+        result[rows, :] = (gate * total).astype(result.dtype)
+        put(chunk).start()
+
     @pl.when(ended)
     def _():
         relay_end(2, o_first)
-        for chunk in range(chunks):
-            arrive(chunk, nearer)
-            if chunk == chunks // 2 - 1:
-                relay_end(2, o_last)
-                relay_end(3, o_first)
-
-    for chunk in range(chunks):
-        arrive(chunk, farther)
-        if chunk % 2:
-            @pl.when(ended)
-            def _():
-                relay_end(3, o_last[chunk // 2 :: chunks // 2])
-
-    for chunk in range(chunks):
-        pass_on(chunk, nearer)
+        arrive(0, nearer)
+        arrive(1, nearer)
+        relay_end(2, o_last)
+        pass_on(0, nearer)
+        pass_on(1, nearer)
+        for shard in middle:
+            outs.complete(shard)
+        first_half(0)
+        first_half(1)
+        relay_end(3, o_first)
+        arrive(2, nearer)
+        arrive(3, nearer)
+
+    arrive(0, farther)
+    arrive(1, farther)
+
+    @pl.when(ended)
+    def _():
+        relay_end(3, o_last[:1])
 
     @pl.when(seated)
     def _():
+        for chunk in range(chunks):
+            pass_on(chunk, nearer)
         pltpu.make_async_copy(own.at[0], own.at[0], own_sems.at[4]).wait()
-
-    last = jnp.where(ended, count - 1 - me, far)
-    middle = (jnp.where(ended, toward, near), jnp.where(ended, low + high - toward, other))
-    for shard in middle:
-        outs.complete(shard)
-
-    def add_up(chunk):
-        taken(slots.at[pl.ds(0, heads), 0, pl.ds(0, block)], sc_sems.at[chunk])
-        gather_up((me,) + middle, chunk)
-
+        for shard in middle:
+            outs.complete(shard)
+        first_half(0)
+        first_half(1)
+
+    arrive(2, farther)
+    arrive(3, farther)
+
+    @pl.when(ended)
+    def _():
+        relay_end(3, o_last[1:])
+        pass_on(2, nearer)
+        pass_on(3, nearer)
+
+    first_half(2)
+    first_half(3)
     for chunk in range(chunks):
         pass_on(chunk, farther)
         if chunk:
-            add_up(chunk - 1)
+            second_half(chunk - 1)
+    second_half(chunks - 1)
     outs.complete(last)
-    for chunk in range(chunks - 1):
-        finish(last, chunk)
-    add_up(chunks - 1)
-    finish(last, chunks - 1)
+    for chunk in range(chunks):
+        finish(chunk)
 
     taken(stage, sent.at[0])
     taken(slots.at[0, 0], sent.at[7])
@@ -1143,10 +1205,10 @@
     def present(self, step, way):
         return self.me >= step if way == 0 else self.me + step < self.count
 
-    def open_way(self, way):
+    def open_way(self, way, chunks=None):
         @pl.when(self.onward(way))
         def _():
-            for chunk in range(self.chunks):
+            for chunk in range(self.chunks) if chunks is None else chunks:
                 self.along(self.me, chunk, way).start()
 
     def relay(self, step, way, chunks=None):
@@ -1213,14 +1275,14 @@
             dma((count, pieces)),
             dma((count,)),
             dma((pieces,)),
-            dma((count, chunks)),
-            dma((count, chunks)),
+            dma((count, chunks + 1)),
+            dma((count, chunks + 1)),
             dma((count, chunks)),
             dma((count, o_chunks)),
             dma((count,)),
             dma((seated, chunks)),
             dma((seated, chunks)),
-            dma((chunks,)),
+            dma((seated, chunks)),
             dma((6,)),
             dma((11,)),
         ],

time: 112 us -> 108 us (0.964)
  Pallas kernels: 110 us -> 106 us
    pallas_call x1, Pallas kernels: 110 us -> 106 us  [by_pair(): pl.pallas_call(functools.partial(by_pair_kernel, sizes, chunks, pieces, o...]
where the time goes in v6:
time: 108 us
  Pallas kernels  106 us (98%)
  local copies, waits for them, and re-layouts  2.06 us (2%)
    pallas_call x1, Pallas kernels, by_pair(): pl.pallas_call(functools.partial(by_pair_kernel, sizes, chunks, pieces, o...  106 us

profile of v6, /device:TPU:0, one launch (start us, length us, event | category | flops | bytes accessed | tf_op | source)
XLA Modules:
  0.0 108.1 jit_solution(9974322499739600241)
XLA Ops:
  0.0 106.0 %by_pair.1 = bf16[512,768]{1,0:T(8,128)(2,1)} custom-call(bf16[512,3072]{1,0:T(8,128)(2,1)} %tokens.1, f32[3,3072]{1,0:T(4,128)} %modulation.1, bf16[768,2,768]{2,1,0:T(2,128)(2,1)} %w_own.1, bf16[512,768]{1,0:T(8,128)(2,1)} %o_own.1, s32[4,4]{1,0:T(4,128)} %pattern.1, s32[1,4]{1,0:T(1,128)} %bitcast.3, s32[4,4]{1,0:T(4,128)} %bitcast.2), custom_call_target="tpu_custom_call" | custom-call | tf_op jit(solution)/shard_map/by_pair/pallas_call | solution.py:1251
  106.0 2.1 %copy.9 = bf16[512,768]{1,0:T(8,128)(2,1)} copy(bf16[512,768]{1,0:T(8,128)(2,1)} %by_pair.1) | data formatting | bytes 1572864

commit v7 on v6

--- a/solution.py
+++ b/solution.py
@@ -930,8 +930,17 @@
         def send(frame, chunk):
             out_push(own, slots, sz_sems, sent, me, frame, chunk, block, low).start()
 
+        def send_part(frame, chunk, first):
+            rows = pl.ds(chunk * block, block)
+            start = pl.multiple_of((me - low) * columns_of + first, size)
+            push(
+                own.at[frame, rows, pl.ds(first, size)],
+                slots.at[0, 0, rows, pl.ds(start, size)],
+                sent.at[6], sz_sems.at[me - low, chunk], "seq", frame,
+            ).start()
+
         def settle(chunk):
-            send(near, chunk)
+            send_part(near, chunk, 0)
             send(other, chunk)
             keep_out(own, slots, own_sems.at[4], me, chunk, block, low).start()
             mine = own.at[me, pl.ds(chunk * block, block)]
@@ -967,6 +976,8 @@
         spatial(me)
         land(far, 2)
         spatial(near)
+        for chunk in range(chunks):
+            send_part(near, chunk, size)
         relay_out(1, None, False)
         far_project(0)
         far_project(1)
@@ -1039,7 +1050,7 @@
         taken(slots.at[0, 0, pl.ds(chunk * block, block)], sc_sems.at[seat - low, chunk])
 
     def put(chunk):
-        rows = pl.ds(chunk * block, block)
+        rows = pl.ds(chunk * 2 * block, 2 * block)
         return pltpu.make_async_copy(result.at[rows], update.at[rows], own_sems.at[5])
 
     nearer = jnp.where(seated, me, toward)
@@ -1061,12 +1072,15 @@
         rows = pl.ds(chunk * block, block)
         partial[0, rows, :] = add_up(chunk, farther, (me,) + middle, partial[0, rows, :])
 
-    def finish(chunk):
-        rows = pl.ds(chunk * block, block)
-        total = add_up(chunk, nearer, (last,), partial[0, rows, :])
-        total = add_up(chunk, farther, (last,), total)
+    def finish(part):
+        hop = lax.rem(head + heads - last // subs, heads)
+        turn = lax.rem(sub + subs - lax.rem(last, subs), subs)
+        rows = pl.ds(part * 2 * block, 2 * block)
+        total = partial[0, rows, :] + jnp.dot(
+            slots[hop, turn, rows, :], o_all[last], preferred_element_type=jnp.float32
+        )
         result[rows, :] = (gate * total).astype(result.dtype)
-        put(chunk).start()
+        put(part).start()
 
     @pl.when(ended)
     def _():
@@ -1118,8 +1132,8 @@
             second_half(chunk - 1)
     second_half(chunks - 1)
     outs.complete(last)
-    for chunk in range(chunks):
-        finish(chunk)
+    for part in range(chunks // 2):
+        finish(part)
 
     taken(stage, sent.at[0])
     taken(slots.at[0, 0], sent.at[7])

time: 108 us -> 107 us (level)
    pallas_call x1, Pallas kernels: 106 us -> 105 us  [by_pair(): pl.pallas_call(functools.partial(by_pair_kernel, sizes, chunks, pieces, o...]
where the time goes in v7:
time: 107 us
  Pallas kernels  105 us (98%)
  local copies, waits for them, and re-layouts  2.06 us (2%)
    pallas_call x1, Pallas kernels, by_pair(): pl.pallas_call(functools.partial(by_pair_kernel, sizes, chunks, pieces, o...  105 us

profile of v7, /device:TPU:0, one launch (start us, length us, event | category | flops | bytes accessed | tf_op | source)
XLA Modules:
  0.0 106.8 jit_solution(2430919212569712669)
XLA Ops:
  0.0 104.7 %by_pair.1 = bf16[512,768]{1,0:T(8,128)(2,1)} custom-call(bf16[512,3072]{1,0:T(8,128)(2,1)} %tokens.1, f32[3,3072]{1,0:T(4,128)} %modulation.1, bf16[768,2,768]{2,1,0:T(2,128)(2,1)} %w_own.1, bf16[512,768]{1,0:T(8,128)(2,1)} %o_own.1, s32[4,4]{1,0:T(4,128)} %pattern.1, s32[1,4]{1,0:T(1,128)} %bitcast.3, s32[4,4]{1,0:T(4,128)} %bitcast.2), custom_call_target="tpu_custom_call" | custom-call | tf_op jit(solution)/shard_map/by_pair/pallas_call | solution.py:1265
  104.7 2.1 %copy.9 = bf16[512,768]{1,0:T(8,128)(2,1)} copy(bf16[512,768]{1,0:T(8,128)(2,1)} %by_pair.1) | data formatting | bytes 1572864
